TPU v7x, 32 devices: a whole 2x2x4 slice. The times are simulated.
32 devices in a mesh: groups: 2 (over y), row: 4 (over x, core), col: 4 (over z).
Axes of the slice: x: 2, y: 2, z: 4, core: 2. Of those that a mesh axis runs over, the one named last changes fastest.
Arguments:
- single: bfloat16 [512, 768], P(('groups', 'row'), 'col'), parts along dimension 0, may hold values from -16 to 16
- pair: bfloat16 [512, 256, 128], P(('groups', 'row'), 'col'), parts along dimension 0, may hold values from -6 to 6
- chain: int32 [512], P('groups'), parts along dimension 0, may hold values from 0 to 7, never falling along the last dimension, each value on 1 to 64 neighbouring positions
- live: int32 [512], P('groups'), parts along dimension 0, may hold values 0 or 1
- step_index: int32 [2], P('groups'), parts along dimension 0, may hold values from 0 to 999
- time_scale: bfloat16 [256, 768], P(None, 'col'), may hold values from -0.375 to 0.375
- time_shift: bfloat16 [256, 768], P(None, 'col'), may hold values from -0.375 to 0.375
- w_query: bfloat16 [768, 768], P(None, 'col'), may hold values from -0.21875 to 0.21875
- w_key: bfloat16 [768, 768], P(None, 'col'), may hold values from -0.21875 to 0.21875
- w_value: bfloat16 [768, 768], P(None, 'col'), may hold values from -0.21875 to 0.21875
- w_gate: bfloat16 [768, 768], P(None, 'col'), may hold values from -0.21875 to 0.21875
- w_out: bfloat16 [768, 768], P(None, 'col'), may hold values from -0.21875 to 0.21875
- pair_gain: float32 [128], replicated, may hold values from 0.1 to 1.9
- bias_weight: bfloat16 [128, 12], replicated, may hold values from -30 to 30
- chain_bias: float32 [2, 12], replicated, may hold values from -4 to 4
- outer_gain: float32 [768], P('col'), may hold values from 0.1 to 1.9
- w_left: float32 [768, 32], P('col'), may hold values from -0.21875 to 0.21875
- w_right: float32 [768, 32], P('col'), may hold values from -0.21875 to 0.21875
- w_outer: bfloat16 [32, 32, 128], replicated, may hold values from -0.1875 to 0.1875
- outer_bias: float32 [128], replicated, may hold values from -4 to 4
- trans_gain: float32 [128], replicated, may hold values from 0.1 to 1.9
- w_in: bfloat16 [128, 1024], replicated, may hold values from -0.5 to 0.5
- w_down: bfloat16 [512, 128], replicated, may hold values from -0.25 to 0.25
Outputs:
- single_out: bfloat16 [512, 768], P(('groups', 'row'), 'col'), parts along dimension 0
- pair_out: bfloat16 [512, 256, 128], P(('groups', 'row'), 'col'), parts along dimension 0
There are 2 independent parts, one for each index of `groups`. A program takes and returns all parts, laid end to end along the dimension named above; an argument that names none is the same for every part. Nothing has to cross between parts.
Inputs may be any that keep to these rules, and one draw needn't show every extreme that they name: chain numbers never fall along the residues.
All inputs are finite; a program needn't handle non-finite values.
Results may differ from a plain program's by a relative error of at most 0.0095.
Values may be sent and summed in bfloat16 or wider, within the bound.
A program may use at most 64 MiB of HBM per device.

v0:
```python
import math

import jax
import jax.numpy as jnp
from jax import lax
from jax.sharding import PartitionSpec as P

EPSILON = 1e-05
MASKED = -1000000000.0


def broadcast(array, axis, root):
    mine = lax.axis_index(axis) == root
    return lax.psum(jnp.where(mine, array, jnp.zeros_like(array)), axis)


def channel_norm(values, gain):
    row_mean = jnp.mean(values, axis=-1, keepdims=True)
    spread = jnp.mean(values * values, axis=-1, keepdims=True) - row_mean * row_mean
    return (values - row_mean) * lax.rsqrt(spread + EPSILON) * gain


def time_embed(step_index, count):
    halfway = count // 2
    ladder = jnp.arange(halfway).astype(jnp.float32)
    freqs = jnp.exp(-math.log(10000.0) * ladder / halfway)
    angles = step_index[0].astype(jnp.float32) * freqs
    return jnp.concatenate([jnp.sin(angles), jnp.cos(angles)])


def head_scores(query_rows, key_rows, bias_terms, head_count):
    query_heads = query_rows.reshape(query_rows.shape[0], head_count, -1)
    key_heads = key_rows.reshape(key_rows.shape[0], head_count, -1)
    raw = jnp.einsum("qhd,khd->hqk", query_heads, key_heads, preferred_element_type=jnp.float32)
    return raw * query_heads.shape[2] ** (-0.5) + bias_terms


def weighted_values(weights_exp, value_rows, head_count):
    value_heads = value_rows.reshape(value_rows.shape[0], head_count, -1).astype(jnp.float32)
    summed = jnp.einsum("hqk,khd->qhd", weights_exp, value_heads, precision=lax.Precision.HIGHEST)
    return summed.reshape(summed.shape[0], -1)


def divide_heads(summed, totals):
    row_count = summed.shape[0]
    head_count = totals.shape[0]
    return (summed.reshape(row_count, head_count, -1) / totals.T[:, :, None]).reshape(row_count, -1)


def transition(flat, gain, w_in, w_down):
    normed = channel_norm(flat, gain).astype(jnp.bfloat16)
    mixed = jnp.dot(normed, w_in, preferred_element_type=jnp.float32)
    halfway = w_down.shape[0]
    hidden = (jax.nn.silu(mixed[:, :halfway]) * mixed[:, halfway:]).astype(jnp.bfloat16)
    return (flat + jnp.dot(hidden, w_down, preferred_element_type=jnp.float32)).astype(jnp.bfloat16)


def body(
    single,
    pair,
    chain,
    live,
    step_index,
    time_scale,
    time_shift,
    w_query,
    w_key,
    w_value,
    w_gate,
    w_out,
    pair_gain,
    bias_weight,
    chain_bias,
    outer_gain,
    w_left,
    w_right,
    w_outer,
    outer_bias,
    trans_gain,
    w_in,
    w_down,
):
    block_rows = single.shape[0]
    model_width = w_query.shape[0]
    head_count = chain_bias.shape[1]
    row_place = lax.axis_index("row")
    col_place = lax.axis_index("col")
    query_start = row_place * block_rows
    key_start = col_place * block_rows
    chain_query = lax.dynamic_slice_in_dim(chain, query_start, block_rows, 0)
    chain_key = lax.dynamic_slice_in_dim(chain, key_start, block_rows, 0)
    live_query = lax.dynamic_slice_in_dim(live, query_start, block_rows, 0).astype(jnp.float32)
    live_keys = lax.dynamic_slice_in_dim(live, key_start, block_rows, 0)
    single_f = single.astype(jnp.float32)
    totals = lax.psum((jnp.sum(single_f, axis=1), jnp.sum(single_f * single_f, axis=1)), "col")
    row_mean = totals[0] / model_width
    inv_std = lax.rsqrt(totals[1] / model_width - row_mean * row_mean + EPSILON)
    embedded = time_embed(step_index, time_scale.shape[0]).astype(jnp.bfloat16)
    mod_scale = jnp.dot(embedded[None], time_scale, preferred_element_type=jnp.float32)[0]
    mod_shift = jnp.dot(embedded[None], time_shift, preferred_element_type=jnp.float32)[0]
    normed = (
        (single_f - row_mean[:, None]) * inv_std[:, None] * (1.0 + mod_scale) + mod_shift
    ).astype(jnp.bfloat16)
    normed_full = lax.all_gather(normed, "col", axis=1, tiled=True)
    query_part = jnp.dot(normed_full, w_query, preferred_element_type=jnp.float32).astype(
        jnp.bfloat16
    )
    key_part = jnp.dot(normed_full, w_key, preferred_element_type=jnp.float32).astype(jnp.bfloat16)
    value_part = jnp.dot(normed_full, w_value, preferred_element_type=jnp.float32).astype(
        jnp.bfloat16
    )
    gate_part = jnp.dot(normed_full, w_gate, preferred_element_type=jnp.float32).astype(
        jnp.bfloat16
    )
    query_full, key_full, value_full, gate_full = (
        lax.all_gather(query_part, "col", axis=1, tiled=True),
        lax.all_gather(key_part, "col", axis=1, tiled=True),
        lax.all_gather(value_part, "col", axis=1, tiled=True),
        lax.all_gather(gate_part, "col", axis=1, tiled=True),
    )
    key_cols, value_cols = (
        broadcast(key_full, "row", col_place),
        broadcast(value_full, "row", col_place),
    )
    pair_normed = channel_norm(pair.astype(jnp.float32), pair_gain).astype(jnp.bfloat16)
    bias_terms = jnp.einsum(
        "qkc,ch->hqk", pair_normed, bias_weight, preferred_element_type=jnp.float32
    )
    same_chain = chain_query[:, None] == chain_key[None, :]
    chain_terms = jnp.where(
        same_chain[None], chain_bias[0][:, None, None], chain_bias[1][:, None, None]
    )
    live_terms = jnp.where(live_keys == 1, 0.0, MASKED).astype(jnp.float32)
    bias_terms = bias_terms + chain_terms + live_terms[None, None, :]
    scores = head_scores(query_full, key_cols, bias_terms, head_count)
    row_top = lax.pmax(jnp.max(scores, axis=2), "col")
    weights_exp = jnp.exp(scores - row_top[:, :, None])
    row_sum, summed = lax.psum(
        (jnp.sum(weights_exp, axis=2), weighted_values(weights_exp, value_cols, head_count)), "col"
    )
    attended = divide_heads(summed, row_sum)
    gated = (jax.nn.sigmoid(gate_full.astype(jnp.float32)) * attended).astype(jnp.bfloat16)
    single_out = (single_f + jnp.dot(gated, w_out, preferred_element_type=jnp.float32)).astype(
        jnp.bfloat16
    )
    updated_single = single_out.astype(jnp.float32)
    gained = updated_single * outer_gain
    joint = lax.psum(
        (
            jnp.sum(updated_single, axis=1),
            jnp.sum(updated_single * updated_single, axis=1),
            jnp.dot(gained, w_left, precision=lax.Precision.HIGHEST),
            jnp.dot(gained, w_right, precision=lax.Precision.HIGHEST),
            jnp.dot(outer_gain[None], w_left, precision=lax.Precision.HIGHEST)[0],
            jnp.dot(outer_gain[None], w_right, precision=lax.Precision.HIGHEST)[0],
        ),
        "col",
    )
    out_mean = joint[0] / model_width
    out_inv = lax.rsqrt(joint[1] / model_width - out_mean * out_mean + EPSILON)
    left_full = out_inv[:, None] * (joint[2] - out_mean[:, None] * joint[4][None, :])
    right_full = out_inv[:, None] * (joint[3] - out_mean[:, None] * joint[5][None, :])
    left_rows = left_full.astype(jnp.bfloat16)
    right_rows = right_full.astype(jnp.bfloat16)
    right_cols = broadcast(right_rows, "row", col_place)
    left_mix = jnp.einsum("ip,pqc->iqc", left_rows, w_outer, preferred_element_type=jnp.float32)
    outer = (
        jnp.einsum(
            "iqc,jq->ijc", left_mix, right_cols.astype(jnp.float32), precision=lax.Precision.HIGHEST
        )
        + outer_bias
    )
    outer = outer * (live_query[:, None] * live_keys.astype(jnp.float32)[None, :])[:, :, None]
    updated = pair.astype(jnp.float32) + outer
    flat = updated.reshape(-1, updated.shape[-1])
    total_rows = flat.shape[0]
    piece_rows = math.gcd(total_rows, 1024)
    pieces = flat.reshape(total_rows // piece_rows, piece_rows, flat.shape[1])
    pair_out = lax.map(lambda piece: transition(piece, trans_gain, w_in, w_down), pieces).reshape(
        pair.shape
    )
    return (single_out, pair_out)


def solution(mesh):
    in_specs = (
        P(("groups", "row"), "col"),
        P(("groups", "row"), "col", None),
        P("groups"),
        P("groups"),
        P("groups"),
        P(None, "col"),
        P(None, "col"),
        P(None, "col"),
        P(None, "col"),
        P(None, "col"),
        P(None, "col"),
        P(None, "col"),
        P(),
        P(),
        P(),
        P("col"),
        P("col", None),
        P("col", None),
        P(),
        P(),
        P(),
        P(),
        P(),
    )
    out_specs = (P(("groups", "row"), "col"), P(("groups", "row"), "col", None))
    return jax.shard_map(body, mesh=mesh, in_specs=in_specs, out_specs=out_specs, check_vma=False)
```

profile of v0, /device:TPU:0, one launch (start us, length us, event | category | flops | bytes accessed | tf_op | source)
XLA Modules:
  0.0 195.5 jit_solution(4892116651313680007)
XLA Ops:
  7.2 0.9 convert_reduce_fusion.1
  8.9 1.0 fusion.64
  10.0 1.1 fusion.65
  11.0 13.5 %all-reduce.1 = (f32[64]{0:T(128)S(1)}, f32[64]{0:T(128)S(1)}) all-reduce(f32[64]{0:T(128)S(1)} %get-tuple-element.40, f32[64]{0:T(128)S(1)} %get-tuple-element.39), channel_id=1, replica_groups=mesh['groups'=2,'row'=4,'col'=4] {'col'}, use_global_device_ids=true, to_apply=%region_3.0 | all-reduce | flops 128 | bytes 1024 | tf_op jit(solution)/shard_map/psum | solution.py:95
  24.5 0.8 fusion.50
  25.4 13.4 %all-gather = bf16[4,192,64]{1,2,0:T(8,128)(2,1)S(1)} all-gather(bf16[1,192,64]{1,2,0:T(8,128)(2,1)S(1)} %fusion.50), channel_id=1, replica_groups=mesh['groups'=2,'row'=4,'col'=4] {'col'}, dimensions={0}, use_global_device_ids=true | all-gather | bytes 122880 | tf_op jit(solution)/shard_map/all_gather | solution.py:104
  38.8 0.1 copy.51
  38.9 0.1 reshape.161
  39.0 1.2 fusion.25
  40.3 13.4 %all-gather.4 = bf16[4,192,64]{1,2,0:T(8,128)(2,1)S(1)} all-gather(bf16[1,192,64]{1,2,0:T(8,128)(2,1)S(1)} %fusion.25), channel_id=1, replica_groups=mesh['groups'=2,'row'=4,'col'=4] {'col'}, dimensions={0}, use_global_device_ids=true | all-gather | bytes 122880 | tf_op jit(solution)/shard_map/all_gather | solution.py:117
  53.6 0.1 copy.56
  53.8 0.1 reshape.176
  53.9 0.2 reshape.157
  54.1 0.7 copy.57
  54.8 0.2 fusion.23
  55.0 13.4 %all-gather.2 = bf16[4,192,64]{1,2,0:T(8,128)(2,1)S(1)} all-gather(bf16[1,192,64]{1,2,0:T(8,128)(2,1)S(1)} %fusion.23), channel_id=1, replica_groups=mesh['groups'=2,'row'=4,'col'=4] {'col'}, dimensions={0}, use_global_device_ids=true | all-gather | bytes 122880 | tf_op jit(solution)/shard_map/all_gather | solution.py:118
  68.4 0.1 copy.53
  68.5 0.1 reshape.173
  68.7 0.8 copy.54
  69.6 0.2 fusion.24
  69.8 13.5 %all-gather.3 = bf16[4,192,64]{1,2,0:T(8,128)(2,1)S(1)} all-gather(bf16[1,192,64]{1,2,0:T(8,128)(2,1)S(1)} %fusion.24), channel_id=1, replica_groups=mesh['groups'=2,'row'=4,'col'=4] {'col'}, dimensions={0}, use_global_device_ids=true | all-gather | bytes 122880 | tf_op jit(solution)/shard_map/all_gather | solution.py:116
  83.4 0.1 reshape.167
  83.5 0.2 reshape.156
  83.7 1.2 convert_reduce_fusion
  85.0 1.5 fusion.26
  86.4 0.2 copy.59
  86.7 0.2 fusion.22
  87.0 13.4 %all-gather.1 = bf16[4,192,64]{1,2,0:T(8,128)(2,1)S(1)} all-gather(bf16[1,192,64]{1,2,0:T(8,128)(2,1)S(1)} %fusion.22), channel_id=1, replica_groups=mesh['groups'=2,'row'=4,'col'=4] {'col'}, dimensions={0}, use_global_device_ids=true | all-gather | bytes 122880 | tf_op jit(solution)/shard_map/all_gather | solution.py:119
  100.4 0.2 copy.52
  100.6 0.2 reshape.178
  101.0 0.1 convolution_bitcast_fusion
  101.3 1.2 fusion.63
  102.5 11.4 %pmax.7 = f32[12,64]{1,0:T(8,128)S(1)} all-reduce(f32[12,64]{1,0:T(8,128)S(1)} %get-tuple-element.77), channel_id=1, replica_groups=mesh['groups'=2,'row'=4,'col'=4] {'col'}, use_global_device_ids=true, to_apply=%region_9.10 | all-reduce | flops 768 | bytes 6144 | tf_op jit(solution)/shard_map/pmax | solution.py:136
  113.9 1.3 fusion.34
  115.2 0.8 copy.61
  116.1 0.1 convolution_bitcast_fusion.1
  116.3 9.0 %psum.96 = f32[64,12]{0,1:T(8,128)S(1)} all-reduce(f32[64,12]{0,1:T(8,128)S(1)} %bitcast.139), channel_id=1, replica_groups=mesh['groups'=2,'row'=4,'col'=4] {'col'}, use_global_device_ids=true, to_apply=%region_12.13 | all-reduce | flops 768 | bytes 6144 | tf_op jit(solution)/shard_map/psum | solution.py:138
  125.4 0.2 div.55
  125.6 0.1 div.56
  125.8 22.7 %all-reduce.6.cloned.1.call-done = f32[64,768]{1,0:T(8,128)} async-done(((f32[64,768]{1,0:T(8,128)}), f32[64,768]{1,0:T(8,128)}) %all-reduce.6.cloned.1.call-update) | async-done | bytes 196624 | tf_op jit(solution)/shard_map/psum | solution.py:138
  148.5 1.3 fusion.44
  149.8 0.2 fusion.42
  150.0 0.2 fusion.43
  150.2 18.1 %all-reduce = (f32[64,32]{0,1:T(8,128)S(1)}, f32[32]{0:T(128)S(1)}, f32[64]{0:T(128)S(1)}, f32[64]{0:T(128)S(1)}, f32[64,32]{0,1:T(8,128)S(1)}, /*index=5*/f32[32]{0:T(128)S(1)}) all-reduce(f32[64,32]{0,1:T(8,128)S(1)} %fusion.42, f32[32]{0:T(128)S(1)} %convolution_bitcast_fusion, ...), channel_id=1, replica_groups=mesh['groups'=2,'row'=4,'col'=4] {'col'}, use_global_device_ids=true, to_apply=%region_20.21 | all-reduce | flops 4288 | bytes 34304 | tf_op jit(solution)/shard_map/psum | solution.py:148
  168.4 5.8 %psum.101 = bf16[64,32]{0,1:T(8,128)(2,1)S(1)} all-reduce(bf16[64,32]{0,1:T(8,128)(2,1)S(1)} %fusion.53), channel_id=1, replica_groups=mesh['groups'=2,'row'=4,'col'=4] {'row'}, use_global_device_ids=true, to_apply=%region_19.20 | all-reduce | flops 2048 | bytes 8192 | tf_op jit(solution)/shard_map/psum | solution.py:14
  174.2 0.4 fusion.35
  174.6 3.4 %convert_add_fusion = f32[64,64,128]{2,1,0:T(8,128)S(1)} fusion(bf16[64,64,128]{2,1,0:T(8,128)(2,1)} %param.26, f32[64,32,128]{2,0,1:T(8,128)S(1)} %fusion.35, f32[64,64]{1,0:T(8,128)S(1)} %broadcast_multiply_fusion.1, f32[128]{0:T(128)S(1)} %copy-done.16, bf16[64,32]{0,1:T(8,128)(2,1)S(1)} %psum.101), kind=kOutput, calls=%fused_computation.21 | convolution fusion | flops 203423744 | bytes 4215296 | tf_op jit(solution)/shard_map/iqc,jq->ijc/dot_general | solution.py:168
  178.1 10.5 %while.10 = (s32[]{:T(128)}, bf16[4,1024,128]{2,1,0:T(8,128)(2,1)}, f32[4,1024,128]{2,1,0:T(8,128)S(1)}, f32[128]{0:T(128)S(1)}, bf16[128,1024]{1,0:T(8,128)(2,1)S(1)}, /*index=5*/bf16[512,128]{1,0:T(8,128)(2,1)S(1)}, s32[]{:T(128)}) while((s32[]{:T(128)}, bf16[4,1024,128]{2,1,0:T(8,128)(2,1)}, f32[4,1024,128]{2,1,0:T(8,128)S(1)}, ...), condition=%wide.region_25.26_spmd, body=%wide.region_22.25_spmd.sunk | while | flops 406981632 | bytes 11175001 | solution.py:179
  178.1 0.2 dynamic-slice_reduce_fusion.2
  178.3 0.2 fusion.100
  178.6 0.8 fusion.101
  179.3 1.4 fusion.102
  180.8 0.2 dynamic-slice_reduce_fusion.2
  181.0 0.2 fusion.100
  181.2 0.8 fusion.101
  182.0 1.4 fusion.102
  183.4 0.2 dynamic-slice_reduce_fusion.2
  183.6 0.2 fusion.100
  183.8 0.8 fusion.101
  184.6 1.4 fusion.102
  186.0 0.2 dynamic-slice_reduce_fusion.2
  186.2 0.2 fusion.100
  186.5 0.8 fusion.101
  187.2 1.4 fusion.102
  (70 shorter events, 1.2 us)
Async XLA Ops:
  7.2 141.3 %copy-start = (bf16[768,192]{0,1:T(8,128)(2,1)S(1)}, bf16[768,192]{0,1:T(8,128)(2,1)}, u32[]{:S(2)}) copy-start(bf16[768,192]{0,1:T(8,128)(2,1)} %param.36) | copy-start | bytes 884740
  7.2 47.6 %copy-start.3 = (bf16[768,192]{0,1:T(8,128)(2,1)S(1)}, bf16[768,192]{0,1:T(8,128)(2,1)}, u32[]{:S(2)}) copy-start(bf16[768,192]{0,1:T(8,128)(2,1)} %param.34) | copy-start | bytes 884740
  7.2 94.1 %all-reduce.8.cloned.1.call-start = ((), (), s32[]{:S(2)}) async-start(), calls=%async_computation.1 | async-start | bytes 786432 | tf_op jit(solution)/shard_map/psum | solution.py:14
  39.0 30.6 %copy-start.4 = (bf16[768,192]{0,1:T(8,128)(2,1)S(1)}, bf16[768,192]{0,1:T(8,128)(2,1)}, u32[]{:S(2)}) copy-start(bf16[768,192]{0,1:T(8,128)(2,1)} %param.32) | copy-start | bytes 884740
  53.9 29.8 %copy-start.2 = (bf16[64,64,128]{2,1,0:T(8,128)(2,1)S(1)}, bf16[64,64,128]{2,1,0:T(8,128)(2,1)}, u32[]{:S(2)}) copy-start(bf16[64,64,128]{2,1,0:T(8,128)(2,1)} %param.26) | copy-start | bytes 3145732
  68.4 16.5 %copy-start.18 = (bf16[128,12]{0,1:T(8,128)(2,1)S(1)}, bf16[128,12]{0,1:T(8,128)(2,1)}, u32[]{:S(2)}) copy-start(bf16[128,12]{0,1:T(8,128)(2,1)} %param.38) | copy-start | bytes 9220
  68.4 16.5 %copy-start.19 = (f32[128]{0:T(128)S(1)}, f32[128]{0:T(128)}, u32[]{:S(2)}) copy-start(f32[128]{0:T(128)} %param.37) | copy-start | bytes 1540
  69.5 79.0 %all-reduce.6.cloned.1.call-start = ((), (), s32[]{:S(2)}) async-start(), calls=%async_computation | async-start | bytes 393216 | tf_op jit(solution)/shard_map/psum | solution.py:138
  83.7 3.0 %copy-start.15 = (f32[2,12]{1,0:T(2,128)S(1)}, f32[2,12]{1,0:T(2,128)}, u32[]{:S(2)}) copy-start(f32[2,12]{1,0:T(2,128)} %param.39) | copy-start | bytes 292
  83.7 3.0 %copy-start.5 = (bf16[768,192]{0,1:T(8,128)(2,1)S(1)}, bf16[768,192]{0,1:T(8,128)(2,1)}, u32[]{:S(2)}) copy-start(bf16[768,192]{0,1:T(8,128)(2,1)} %param.35) | copy-start | bytes 884740
  84.9 15.8 %copy-start.13 = (s32[256]{0:T(256)S(1)}, s32[256]{0:T(256)}, u32[]{:S(2)}) copy-start(s32[256]{0:T(256)} %param.27) | copy-start | bytes 3076
  84.9 15.9 %copy-start.14 = (s32[256]{0:T(256)S(1)}, s32[256]{0:T(256)}, u32[]{:S(2)}) copy-start(s32[256]{0:T(256)} %param.28) | copy-start | bytes 3076
  85.0 16.1 %copy-start.8 = (f32[192,32]{0,1:T(8,128)S(1)}, f32[192,32]{0,1:T(8,128)}, u32[]{:S(2)}) copy-start(f32[192,32]{0,1:T(8,128)} %param.41) | copy-start | bytes 73732
  85.0 16.1 %copy-start.11 = (f32[192]{0:T(256)S(1)}, f32[192]{0:T(256)}, u32[]{:S(2)}) copy-start(f32[192]{0:T(256)} %param.40) | copy-start | bytes 2308
  100.4 15.7 %copy-start.9 = (f32[192,32]{0,1:T(8,128)S(1)}, f32[192,32]{0,1:T(8,128)}, u32[]{:S(2)}) copy-start(f32[192,32]{0,1:T(8,128)} %param.42) | copy-start | bytes 73732
  101.3 47.2 %copy-start.7 = (bf16[64,192]{1,0:T(8,128)(2,1)S(1)}, bf16[64,192]{1,0:T(8,128)(2,1)}, u32[]{:S(2)}) copy-start(bf16[64,192]{1,0:T(8,128)(2,1)} %param.25) | copy-start | bytes 73732
  116.1 58.1 %copy-start.6 = (bf16[32,32,128]{2,1,0:T(8,128)(2,1)S(1)}, bf16[32,32,128]{2,1,0:T(8,128)(2,1)}, u32[]{:S(2)}) copy-start(bf16[32,32,128]{2,1,0:T(8,128)(2,1)} %param.43) | copy-start | bytes 786436
  125.6 49.0 %copy-start.16 = (f32[128]{0:T(128)S(1)}, f32[128]{0:T(128)}, u32[]{:S(2)}) copy-start(f32[128]{0:T(128)} %param.44) | copy-start | bytes 1540
  149.8 28.3 %copy-start.10 = (bf16[64,192]{1,0:T(8,128)(2,1)}, bf16[64,192]{1,0:T(8,128)(2,1)S(1)}, u32[]{:S(2)}) copy-start(bf16[64,192]{1,0:T(8,128)(2,1)S(1)} %get-tuple-element.79) | copy-start | bytes 73732
  174.6 3.5 %copy-start.1 = (bf16[128,1024]{1,0:T(8,128)(2,1)S(1)}, bf16[128,1024]{1,0:T(8,128)(2,1)}, u32[]{:S(2)}) copy-start(bf16[128,1024]{1,0:T(8,128)(2,1)} %param.46) | copy-start | bytes 786436
  174.6 3.5 %copy-start.12 = (f32[128]{0:T(128)S(1)}, f32[128]{0:T(128)}, u32[]{:S(2)}) copy-start(f32[128]{0:T(128)} %param.45) | copy-start | bytes 1540
  174.6 3.5 %copy-start.17 = (bf16[512,128]{1,0:T(8,128)(2,1)S(1)}, bf16[512,128]{1,0:T(8,128)(2,1)}, u32[]{:S(2)}) copy-start(bf16[512,128]{1,0:T(8,128)(2,1)} %param.47) | copy-start | bytes 393220
Sparse Core Ops, SparseCore 0:
  69.6 31.1 all-reduce.7
  116.2 32.2 all-reduce.5
where the time goes:
time: 196 us; the launch traced here: 195 us
  blocking collectives  125 us (64%)
  waiting for transfers between devices  22.8 us (12%)
  matrix products  22.4 us (11%)
  between operations  15.3 us (8%)
  other arithmetic  5.32 us (3%)
  local copies, waits for them, and re-layouts  4.85 us (2%)
    psum x1, waiting for transfers between devices, body(): lax.psum((jnp.sum(weights_exp, axis=2), weighted_values(weights_exp, valu...  22.7 us
    psum x1, blocking collectives, body(): lax.psum((jnp.sum(updated_single, axis=1), jnp.sum(updated_single * updat...  18.1 us
    psum x1, blocking collectives, body(): lax.psum((jnp.sum(single_f, axis=1), jnp.sum(single_f * single_f, axis=1)...  13.5 us
    all_gather x1, blocking collectives, body(): lax.all_gather(query_part, 'col', axis=1, tiled=True)  13.5 us
    all_gather x1, blocking collectives, body(): normed_full = lax.all_gather(normed, 'col', axis=1, tiled=True)  13.4 us
    all_gather x1, blocking collectives, body(): lax.all_gather(value_part, 'col', axis=1, tiled=True)  13.4 us
    all_gather x1, blocking collectives, body(): lax.all_gather(gate_part, 'col', axis=1, tiled=True)  13.4 us
    all_gather x1, blocking collectives, body(): lax.all_gather(key_part, 'col', axis=1, tiled=True)  13.4 us
  transfers between devices with their start and end apart: 2, of which 1 were waited for; matrix products, arithmetic and copies ran while one was open for 3% of the time, Pallas kernels for 0%

commit v1 on v0

--- a/solution.py
+++ b/solution.py
@@ -1,8 +1,11 @@
+import functools
 import math
 
 import jax
 import jax.numpy as jnp
 from jax import lax
+from jax.experimental import pallas as pl
+from jax.experimental.pallas import tpu as pltpu
 from jax.sharding import PartitionSpec as P
 
 EPSILON = 1e-05
@@ -182,6 +185,495 @@
     return (single_out, pair_out)
 
 
+MESH_ID = pl.DeviceIdType.MESH
+
+
+def attention_kernel(
+    row_count,
+    col_count,
+    head_size,
+    single_ref,
+    embedded_ref,
+    scale_ref,
+    shift_ref,
+    query_w_ref,
+    key_w_ref,
+    value_w_ref,
+    gate_w_ref,
+    out_w_ref,
+    bias_ref,
+    gain_ref,
+    factors_ref,
+    single_out_ref,
+    left_ref,
+    right_ref,
+    singles,
+    mods,
+    biases,
+    keys_values,
+    gates,
+    left_parts,
+    right_parts,
+    col_send,
+    col_recv,
+    row_send,
+    row_recv,
+    right_send,
+    right_recv,
+):
+    row_place = lax.axis_index("row")
+    col_place = lax.axis_index("col")
+    rows, width = single_ref.shape
+    model_width = query_w_ref.shape[0]
+    factor = left_ref.shape[1]
+    head_count = width // head_size
+
+    def col_peer(step):
+        return {"col": lax.rem(col_place + step, col_count)}
+
+    def row_peer(step):
+        return {"row": lax.rem(row_place + step, row_count)}
+
+    def copy(source, target, send, recv, device):
+        return pltpu.make_async_remote_copy(
+            src_ref=source,
+            dst_ref=target,
+            send_sem=send,
+            recv_sem=recv,
+            device_id=device,
+            device_id_type=MESH_ID,
+        )
+
+    barrier = pltpu.get_barrier_semaphore()
+    for row_step in range(row_count):
+        for col_step in range(col_count):
+            if row_step or col_step:
+                pl.semaphore_signal(
+                    barrier,
+                    inc=1,
+                    device_id=row_peer(row_step) | col_peer(col_step),
+                    device_id_type=MESH_ID,
+                )
+    embedded = embedded_ref[...]
+    mod_scale = jnp.dot(embedded, scale_ref[...], preferred_element_type=jnp.float32)
+    mod_shift = jnp.dot(embedded, shift_ref[...], preferred_element_type=jnp.float32)
+    mods[col_place, 0] = mod_scale[:8]
+    mods[col_place, 1] = mod_shift[:8]
+    singles[col_place] = single_ref[...]
+    pl.semaphore_wait(barrier, row_count * col_count - 1)
+
+    first = []
+    bias_copies = []
+    for step in range(1, col_count):
+        peer = col_peer(step)
+        first.append(
+            copy(
+                single_ref,
+                singles.at[col_place],
+                col_send.at[0, step],
+                col_recv.at[0, step],
+                peer,
+            )
+        )
+        first.append(
+            copy(
+                mods.at[col_place],
+                mods.at[col_place],
+                col_send.at[1, step],
+                col_recv.at[1, step],
+                peer,
+            )
+        )
+        bias_copies.append(
+            copy(
+                bias_ref.at[lax.rem(col_place + step, col_count)],
+                biases.at[col_place],
+                col_send.at[2, step],
+                col_recv.at[2, step],
+                peer,
+            )
+        )
+    for each in first:
+        each.start()
+    for each in bias_copies:
+        each.start()
+    biases[col_place] = bias_ref[col_place]
+    for each in first:
+        each.wait()
+
+    total = jnp.zeros((rows, 1), jnp.float32)
+    squares = jnp.zeros((rows, 1), jnp.float32)
+    for block in range(col_count):
+        piece = singles[block].astype(jnp.float32)
+        total = total + jnp.sum(piece, axis=1, keepdims=True)
+        squares = squares + jnp.sum(piece * piece, axis=1, keepdims=True)
+    mean = total / model_width
+    inv = lax.rsqrt(squares / model_width - mean * mean + EPSILON)
+    query = jnp.zeros((rows, width), jnp.float32)
+    key = jnp.zeros((rows, width), jnp.float32)
+    value = jnp.zeros((rows, width), jnp.float32)
+    gate = jnp.zeros((rows, width), jnp.float32)
+    for block in range(col_count):
+        piece = singles[block].astype(jnp.float32)
+        normed = (piece - mean) * inv * (1.0 + mods[block, 0, 0:1]) + mods[block, 1, 0:1]
+        normed = normed.astype(jnp.bfloat16)
+        span = pl.ds(block * width, width)
+        key += jnp.dot(normed, key_w_ref[span, :], preferred_element_type=jnp.float32)
+        value += jnp.dot(normed, value_w_ref[span, :], preferred_element_type=jnp.float32)
+        query += jnp.dot(normed, query_w_ref[span, :], preferred_element_type=jnp.float32)
+        gate += jnp.dot(normed, gate_w_ref[span, :], preferred_element_type=jnp.float32)
+    keys_values[row_place, 0] = key.astype(jnp.bfloat16)
+    keys_values[row_place, 1] = value.astype(jnp.bfloat16)
+    second = [
+        copy(
+            keys_values.at[row_place],
+            keys_values.at[row_place],
+            row_send.at[step],
+            row_recv.at[step],
+            row_peer(step),
+        )
+        for step in range(1, row_count)
+    ]
+    for each in second:
+        each.start()
+    opened = jax.nn.sigmoid(gate.astype(jnp.bfloat16).astype(jnp.float32))
+    query = query.astype(jnp.bfloat16)
+    lane = lax.broadcasted_iota(jnp.int32, (rows, width), 1)
+    masks = [
+        (lane >= head * head_size) & (lane < (head + 1) * head_size) for head in range(head_count)
+    ]
+    query_heads = jnp.concatenate(
+        [jnp.where(mask, query, jnp.zeros_like(query)) for mask in masks], axis=0
+    )
+    for each in bias_copies:
+        each.wait()
+    for each in second:
+        each.wait()
+    scores = [
+        lax.dot_general(
+            query_heads,
+            keys_values[block, 0],
+            (((1,), (1,)), ((), ())),
+            preferred_element_type=jnp.float32,
+        )
+        * head_size ** (-0.5)
+        + biases[block]
+        for block in range(row_count)
+    ]
+    top = functools.reduce(jnp.maximum, [jnp.max(s, axis=1, keepdims=True) for s in scores])
+    weights = [jnp.exp(s - top) for s in scores]
+    weight_sum = sum(jnp.sum(w, axis=1, keepdims=True) for w in weights)
+    summed = sum(
+        jnp.dot(
+            weights[block].astype(jnp.bfloat16),
+            keys_values[block, 1],
+            preferred_element_type=jnp.float32,
+        )
+        for block in range(row_count)
+    )
+    summed = summed / weight_sum
+    attended = sum(
+        jnp.where(masks[head], summed[head * rows : (head + 1) * rows], 0.0)
+        for head in range(head_count)
+    )
+    gates[col_place] = (opened * attended).astype(jnp.bfloat16)
+    third = [
+        copy(
+            gates.at[col_place],
+            gates.at[col_place],
+            col_send.at[3, step],
+            col_recv.at[3, step],
+            col_peer(step),
+        )
+        for step in range(1, col_count)
+    ]
+    for each in third:
+        each.start()
+    for each in third:
+        each.wait()
+    mixed = single_ref[...].astype(jnp.float32)
+    for block in range(col_count):
+        mixed += jnp.dot(
+            gates[block],
+            out_w_ref[pl.ds(block * width, width), :],
+            preferred_element_type=jnp.float32,
+        )
+    single_out = mixed.astype(jnp.bfloat16)
+    single_out_ref[...] = single_out
+    updated = single_out.astype(jnp.float32)
+    gain = gain_ref[...]
+    stacked = jnp.concatenate([updated * gain, jnp.broadcast_to(gain, (8, width))], axis=0)
+    products = jnp.dot(
+        stacked,
+        factors_ref[...],
+        precision=lax.Precision.HIGHEST,
+        preferred_element_type=jnp.float32,
+    )
+    place = lax.broadcasted_iota(jnp.int32, (rows, products.shape[1]), 1)
+    left_parts[col_place, pl.ds(0, rows), :] = jnp.where(
+        place == 2 * factor,
+        jnp.sum(updated, axis=1, keepdims=True),
+        jnp.where(
+            place == 2 * factor + 1,
+            jnp.sum(updated * updated, axis=1, keepdims=True),
+            products[:rows],
+        ),
+    )
+    left_parts[col_place, pl.ds(rows, 8), :] = products[rows:]
+    fourth = [
+        copy(
+            left_parts.at[col_place],
+            left_parts.at[col_place],
+            col_send.at[4, step],
+            col_recv.at[4, step],
+            col_peer(step),
+        )
+        for step in range(1, col_count)
+    ]
+    right_copies = [
+        copy(
+            left_parts.at[col_place],
+            right_parts.at[col_place],
+            right_send.at[step],
+            right_recv.at[col_place],
+            row_peer(step) | {"col": row_place},
+        )
+        for step in range(row_count)
+    ]
+    diagonal = row_place == col_place
+    for each in fourth:
+        each.start()
+    for step in range(1, row_count):
+        right_copies[step].start()
+
+    @pl.when(jnp.logical_not(diagonal))
+    def _():
+        right_copies[0].start()
+
+    @pl.when(diagonal)
+    def _():
+        right_parts[col_place] = left_parts[col_place]
+
+    for each in fourth:
+        each.wait()
+
+    def finish(parts):
+        joint = parts[0]
+        for block in range(1, col_count):
+            joint = joint + parts[block]
+        body_rows = joint[:rows]
+        out_mean = body_rows[:, 2 * factor : 2 * factor + 1] / model_width
+        out_square = body_rows[:, 2 * factor + 1 : 2 * factor + 2] / model_width
+        out_inv = lax.rsqrt(out_square - out_mean * out_mean + EPSILON)
+        return out_inv * (body_rows - out_mean * joint[rows : rows + 1])
+
+    left_ref[...] = finish(left_parts)[:, :factor].astype(jnp.bfloat16)
+    for block in range(col_count):
+
+        @pl.when(jnp.logical_not(diagonal & (col_place == block)))
+        def _():
+            copy(
+                left_parts.at[block],
+                right_parts.at[block],
+                right_send.at[0],
+                right_recv.at[block],
+                row_peer(0),
+            ).wait_recv()
+
+    right_ref[...] = finish(right_parts)[:, factor : 2 * factor].astype(jnp.bfloat16)
+    for step in range(1, row_count):
+        right_copies[step].wait_send()
+
+    @pl.when(jnp.logical_not(diagonal))
+    def _():
+        right_copies[0].wait_send()
+
+
+def pair_kernel(
+    live_ref,
+    pair_ref,
+    mix_ref,
+    right_ref,
+    live_keys_ref,
+    outer_bias_ref,
+    gain_ref,
+    w_in_ref,
+    w_down_ref,
+    out_ref,
+    flat_ref,
+):
+    block_rows, key_rows, channels = pair_ref.shape
+    start = pl.program_id(0) * block_rows
+    right = right_ref[...]
+    right_twice = jnp.concatenate([right, right], axis=1)
+    live_keys = live_keys_ref[...]
+    outer_bias = outer_bias_ref[...]
+    for place in range(block_rows):
+        mix = mix_ref[place]
+        high = mix.astype(jnp.bfloat16)
+        low = (mix - high.astype(jnp.float32)).astype(jnp.bfloat16)
+        outer = jnp.dot(
+            right_twice,
+            jnp.concatenate([high, low], axis=0),
+            preferred_element_type=jnp.float32,
+        )
+        outer = (outer + outer_bias) * (live_keys * live_ref[start + place])
+        flat_ref[pl.ds(place * key_rows, key_rows), :] = pair_ref[place].astype(jnp.float32) + outer
+    flat = flat_ref[...]
+    normed = channel_norm(flat, gain_ref[...]).astype(jnp.bfloat16)
+    hidden_width = w_down_ref.shape[0]
+    chunk = math.gcd(hidden_width, 256)
+    result = flat
+    for first in range(0, hidden_width, chunk):
+        gate = jnp.dot(normed, w_in_ref[:, first : first + chunk], preferred_element_type=jnp.float32)
+        up = jnp.dot(
+            normed,
+            w_in_ref[:, hidden_width + first : hidden_width + first + chunk],
+            preferred_element_type=jnp.float32,
+        )
+        half = gate * 0.5
+        hidden = ((half + half * jnp.tanh(half)) * up).astype(jnp.bfloat16)
+        result = result + jnp.dot(
+            hidden, w_down_ref[first : first + chunk, :], preferred_element_type=jnp.float32
+        )
+    out_ref[...] = result.astype(jnp.bfloat16).reshape(out_ref.shape)
+
+
+def fast_body(
+    row_count,
+    col_count,
+    single,
+    pair,
+    chain,
+    live,
+    step_index,
+    time_scale,
+    time_shift,
+    w_query,
+    w_key,
+    w_value,
+    w_gate,
+    w_out,
+    pair_gain,
+    bias_weight,
+    chain_bias,
+    outer_gain,
+    w_left,
+    w_right,
+    w_outer,
+    outer_bias,
+    trans_gain,
+    w_in,
+    w_down,
+):
+    rows, width = single.shape
+    model_width = w_query.shape[0]
+    head_count = chain_bias.shape[1]
+    head_size = model_width // head_count
+    local_heads = head_count // col_count
+    factor = w_left.shape[1]
+    channels = pair.shape[2]
+    query_start = lax.axis_index("row") * rows
+    key_start = lax.axis_index("col") * rows
+    chain_query = lax.dynamic_slice_in_dim(chain, query_start, rows, 0)
+    chain_key = lax.dynamic_slice_in_dim(chain, key_start, rows, 0)
+    live_query = lax.dynamic_slice_in_dim(live, query_start, rows, 0).astype(jnp.float32)
+    live_keys = lax.dynamic_slice_in_dim(live, key_start, rows, 0)
+    embedded = time_embed(step_index, time_scale.shape[0]).astype(jnp.bfloat16)
+    embedded = jnp.broadcast_to(embedded[None], (16, embedded.shape[0]))
+    pair_normed = channel_norm(pair.astype(jnp.float32), pair_gain).astype(jnp.bfloat16)
+    bias_terms = jnp.einsum(
+        "qkc,ch->hqk", pair_normed, bias_weight, preferred_element_type=jnp.float32
+    )
+    same_chain = chain_query[:, None] == chain_key[None, :]
+    chain_terms = jnp.where(
+        same_chain[None], chain_bias[0][:, None, None], chain_bias[1][:, None, None]
+    )
+    live_terms = jnp.where(live_keys == 1, 0.0, MASKED).astype(jnp.float32)
+    bias_terms = bias_terms + chain_terms + live_terms[None, None, :]
+    bias_terms = bias_terms.reshape(col_count, local_heads * rows, rows)
+    lanes = 128 * pl.cdiv(2 * factor + 2, 128)
+    factors = jnp.concatenate(
+        [w_left, w_right, jnp.zeros((width, lanes - 2 * factor), jnp.float32)], axis=1
+    )
+    vmem = pl.BlockSpec(memory_space=pltpu.VMEM)
+    bf16, f32 = jnp.bfloat16, jnp.float32
+    single_out, left, right = pl.pallas_call(
+        functools.partial(attention_kernel, row_count, col_count, head_size),
+        out_shape=(
+            jax.ShapeDtypeStruct((rows, width), bf16),
+            jax.ShapeDtypeStruct((rows, factor), bf16),
+            jax.ShapeDtypeStruct((rows, factor), bf16),
+        ),
+        in_specs=[vmem] * 12,
+        out_specs=(vmem, vmem, vmem),
+        scratch_shapes=[
+            pltpu.VMEM((col_count, rows, width), bf16),
+            pltpu.VMEM((col_count, 2, 8, width), f32),
+            pltpu.VMEM((col_count, local_heads * rows, rows), f32),
+            pltpu.VMEM((row_count, 2, rows, width), bf16),
+            pltpu.VMEM((col_count, rows, width), bf16),
+            pltpu.VMEM((col_count, rows + 8, lanes), f32),
+            pltpu.VMEM((col_count, rows + 8, lanes), f32),
+            pltpu.SemaphoreType.DMA((5, col_count)),
+            pltpu.SemaphoreType.DMA((5, col_count)),
+            pltpu.SemaphoreType.DMA((row_count,)),
+            pltpu.SemaphoreType.DMA((row_count,)),
+            pltpu.SemaphoreType.DMA((row_count,)),
+            pltpu.SemaphoreType.DMA((col_count,)),
+        ],
+        compiler_params=pltpu.CompilerParams(collective_id=0, has_side_effects=True),
+        name="attention",
+    )(
+        single,
+        embedded,
+        time_scale,
+        time_shift,
+        w_query,
+        w_key,
+        w_value,
+        w_gate,
+        w_out,
+        bias_terms,
+        outer_gain[None],
+        factors,
+    )
+    left_mix = jnp.einsum("ip,pqc->iqc", left, w_outer, preferred_element_type=jnp.float32)
+    live_lanes = jnp.broadcast_to(live_keys.astype(jnp.float32)[:, None], (rows, channels))
+    block = math.gcd(rows, 8)
+    hidden = w_down.shape[0]
+    pair_out = pl.pallas_call(
+        pair_kernel,
+        grid=(rows // block,),
+        out_shape=jax.ShapeDtypeStruct(pair.shape, bf16),
+        in_specs=[
+            pl.BlockSpec(memory_space=pltpu.SMEM),
+            pl.BlockSpec((block, rows, channels), lambda i: (i, 0, 0)),
+            pl.BlockSpec((block, factor, channels), lambda i: (i, 0, 0)),
+            pl.BlockSpec((rows, factor), lambda i: (0, 0)),
+            pl.BlockSpec((rows, channels), lambda i: (0, 0)),
+            pl.BlockSpec((1, channels), lambda i: (0, 0)),
+            pl.BlockSpec((1, channels), lambda i: (0, 0)),
+            pl.BlockSpec((channels, 2 * hidden), lambda i: (0, 0)),
+            pl.BlockSpec((hidden, channels), lambda i: (0, 0)),
+        ],
+        out_specs=pl.BlockSpec((block, rows, channels), lambda i: (i, 0, 0)),
+        scratch_shapes=[pltpu.VMEM((block * rows, channels), f32)],
+        name="transition",
+    )(
+        live_query,
+        pair,
+        left_mix,
+        right,
+        live_lanes,
+        outer_bias[None],
+        trans_gain[None],
+        w_in,
+        w_down,
+    )
+    return (single_out, pair_out)
+
+
 def solution(mesh):
     in_specs = (
         P(("groups", "row"), "col"),
@@ -209,4 +701,12 @@
         P(),
     )
     out_specs = (P(("groups", "row"), "col"), P(("groups", "row"), "col", None))
-    return jax.shard_map(body, mesh=mesh, in_specs=in_specs, out_specs=out_specs, check_vma=False)
+    row_count, col_count = mesh.shape["row"], mesh.shape["col"]
+
+    def chosen(*args):
+        head_count = args[14].shape[1]
+        if row_count == col_count and head_count % col_count == 0:
+            return fast_body(row_count, col_count, *args)
+        return body(*args)
+
+    return jax.shard_map(chosen, mesh=mesh, in_specs=in_specs, out_specs=out_specs, check_vma=False)

time: 196 us -> 69.8 us (0.36)
  blocking collectives: 125 us -> 0 us
  Pallas kernels: 0 us -> 49.4 us
  waiting for transfers between devices: 22.8 us -> 0 us
  matrix products: 22.4 us -> 2.27 us
  between operations: 15.3 us -> 1.5 us
  local copies, waits for them, and re-layouts: 4.85 us -> 10.8 us
    all_gather x5 -> x0, blocking collectives: 67 us -> none  [the longest x1 13.5 us: body(): lax.all_gather(query_part, 'col', axis=1, tiled=True)]
    pallas_call x0 -> x2, Pallas kernels: none -> 49.4 us  [the longest x1 39.4 us: fast_body(): pl.pallas_call(functools.partial(attention_kernel, row_count, col_count,...]
    psum x4 -> x0, blocking collectives: 46.4 us -> none  [the longest x1 18.1 us: body(): lax.psum((jnp.sum(updated_single, axis=1), jnp.sum(updated_single * updat...]
    psum x2 -> x0, waiting for transfers between devices: 22.7 us -> none  [the longest x1 22.7 us: body(): lax.psum((jnp.sum(weights_exp, axis=2), weighted_values(weights_exp, valu...]
    dot_general x24 -> x2, matrix products: 22.4 us -> 2.27 us  [the longest x1 1.28 us: fast_body(): jnp.einsum('qkc,ch->hqk', pair_normed, bias_weight, preferred_element_typ...]
    pmax x1 -> x0, blocking collectives: 11.4 us -> none  [body(): row_top = lax.pmax(jnp.max(scores, axis=2), 'col')]
    unnamed x42 -> x40, local copies, waits for them, and re-layouts: 0.38 us -> 6.99 us
  transfers between devices with their start and end apart: 2 -> 0, of which waited for: 1 -> 0; matrix products, arithmetic and copies ran while one was open for 3% -> 0% of each run, Pallas kernels for 0% -> 0%
where the time goes in v1:
time: 69.8 us; the launch traced here: 69.4 us
  Pallas kernels  49.4 us (71%)
  local copies, waits for them, and re-layouts  10.8 us (15%)
  other arithmetic  5.42 us (8%)
  matrix products  2.27 us (3%)
  between operations  1.5 us (2%)
    pallas_call x1, Pallas kernels, fast_body(): pl.pallas_call(functools.partial(attention_kernel, row_count, col_count,...  39.4 us
    pallas_call x1, Pallas kernels, fast_body(): pl.pallas_call(pair_kernel, grid=(rows // block,), out_shape=jax.ShapeDty...  9.96 us
    unnamed x40, local copies, waits for them, and re-layouts  6.99 us
    reduce_sum x1, other arithmetic, channel_norm(): row_mean = jnp.mean(values, axis=-1, keepdims=True)  2.38 us
    dot_general x1, local copies, waits for them, and re-layouts, fast_body(): jnp.einsum('ip,pqc->iqc', left, w_outer, preferred_element_type=jnp.float32)  1.59 us
    convert_element_type x1, other arithmetic, fast_body(): live_keys.astype(jnp.float32)[:, None]  1.41 us

profile of v1, /device:TPU:0, one launch (start us, length us, event | category | flops | bytes accessed | tf_op | source)
XLA Modules:
  0.0 69.4 jit_solution(11062294883440348507)
XLA Ops:
  0.6 0.0 copy-start
  0.6 0.0 copy-start.1
  0.7 0.0 copy-start.12
  0.7 0.0 copy-start.14
  0.7 0.0 copy-start.13
  0.7 1.4 %dynamic-slice_convert_fusion.1 = (f32[64]{0:T(128)S(1)}, f32[64]{0:T(128)}, s32[64]{0:T(128)S(1)}, s32[64]{0:T(128)S(1)}) fusion(s32[256]{0:T(256)} %param.26, s32[]{:T(128)S(6)} %select_n.17, s32[]{:T(128)S(6)} %select_n.16, s32[256]{0:T(256)} %param.25), kind=kLoop, calls=%fused_computation.29 | loop fusion | flops 128 | bytes 2056 | tf_op jit(solution)/shard_map/convert_element_type | solution.py:642
  2.1 0.1 broadcast_compare_fusion
  2.2 0.8 %compare_select_fusion = f32[64]{0:T(128)S(1)} fusion(s32[256]{0:T(256)} %param.26, s32[]{:T(128)S(6)} %select_n.17), kind=kLoop, calls=%fused_computation.21 | loop fusion | flops 128 | bytes 516 | tf_op jit(solution)/shard_map/jit(_where)/select_n | solution.py:592
  2.9 2.4 %convert_reduce_fusion = (f32[64,64]{1,0:T(8,128)S(1)}, f32[64,64]{1,0:T(8,128)S(1)}) fusion(bf16[64,64,128]{2,1,0:T(8,128)(2,1)} %pair_ref.1), kind=kLoop, calls=%fused_computation.2 | loop fusion | flops 2088960 | bytes 1081344 | tf_op jit(solution)/shard_map/reduce_sum | solution.py:21
  5.3 0.0 copy-done.12
  5.4 0.0 copy-done.1
  5.4 0.0 copy-done.14
  5.4 0.0 copy-done.13
  5.4 1.3 %fusion.5 = f32[12,64,64]{2,0,1:T(8,128)S(1)} fusion(bf16[64,64,128]{2,1,0:T(8,128)(2,1)S(1)} %copy-done.1, f32[128]{0:T(128)S(1)} %copy-done.14, f32[64,64]{1,0:T(8,128)S(1)} %get-tuple-element.11, f32[64,64]{1,0:T(8,128)S(1)} %get-tuple-element.10, f32[64]{0:T(128)S(1)} %compare_select_fusion, f32[12]{0:T(128)S(1)} %get-tuple-element.17, ...), kind=kOutput, calls=%fused_computation.9 | convolution fusion | flops 15351808 | bytes 1285984 | tf_op jit(solution)/shard_map/qkc,ch->hqk/dot_general | solution.py:585
  6.7 0.0 copy-start.2
  6.7 0.0 copy-start.3
  6.7 0.0 copy-start.4
  6.7 0.9 %copy.25 = f32[12,64,64]{2,1,0:T(8,128)} copy(f32[12,64,64]{2,0,1:T(8,128)S(1)} %fusion.5) | data formatting | bytes 393216 | tf_op jit(solution)/shard_map/add | solution.py:593
  7.5 0.0 copy-start.5
  8.3 0.6 broadcast_in_dim.67.embedded_ref
  8.9 0.0 copy-done.2
  8.9 0.9 %copy.30.query_w_ref = bf16[768,192]{1,0:T(8,128)(2,1)} copy(bf16[768,192]{0,1:T(8,128)(2,1)S(1)} %copy-done.2) | data formatting | bytes 589824 | tf_op args[7]
  9.8 0.0 copy-done.3
  9.8 0.0 copy-start.6
  9.8 0.9 %copy.31.key_w_ref = bf16[768,192]{1,0:T(8,128)(2,1)} copy(bf16[768,192]{0,1:T(8,128)(2,1)S(1)} %copy-done.3) | data formatting | bytes 589824 | tf_op args[8]
  10.8 0.0 copy-done.4
  10.8 0.0 copy-start.10
  10.8 0.0 copy-start.11
  10.8 0.9 %copy.32.value_w_ref = bf16[768,192]{1,0:T(8,128)(2,1)} copy(bf16[768,192]{0,1:T(8,128)(2,1)S(1)} %copy-done.4) | data formatting | bytes 589824 | tf_op args[9]
  11.7 0.0 copy-done.5
  11.7 0.0 copy-start.7
  11.7 0.0 copy-start.8
  11.7 0.9 %copy.33.gate_w_ref = bf16[768,192]{1,0:T(8,128)(2,1)} copy(bf16[768,192]{0,1:T(8,128)(2,1)S(1)} %copy-done.5) | data formatting | bytes 589824 | tf_op args[10]
  12.6 0.0 copy-done.6
  12.6 0.9 %copy.34.out_w_ref = bf16[768,192]{1,0:T(8,128)(2,1)} copy(bf16[768,192]{0,1:T(8,128)(2,1)S(1)} %copy-done.6) | data formatting | bytes 589824 | tf_op args[11]
  13.6 0.0 copy-done.10
  13.6 0.1 copy.26
  13.7 0.0 copy-done.11
  13.7 0.1 copy.27
  13.8 0.1 pad.2.clone
  13.9 0.7 %maximum_maximum_fusion.factors_ref = f32[192,128]{1,0:T(8,128)} fusion(f32[192,32]{1,0:T(8,128)S(1)} %copy.27, f32[192,32]{1,0:T(8,128)S(1)} %copy.26, f32[128]{0:T(128)S(1)} %pad.2.clone), kind=kLoop, calls=%fused_computation.15 | loop fusion | flops 49152 | bytes 147968 | tf_op jit(solution)/shard_map/concatenate | solution.py:596
  14.6 0.0 copy-done.7
  14.6 0.8 %copy.28.scale_ref = bf16[256,192]{1,0:T(8,128)(2,1)} copy(bf16[256,192]{0,1:T(8,128)(2,1)S(1)} %copy-done.7) | data formatting | bytes 196608 | tf_op args[5]
  15.3 0.0 copy-done.8
  15.3 0.7 %copy.29.shift_ref = bf16[256,192]{1,0:T(8,128)(2,1)} copy(bf16[256,192]{0,1:T(8,128)(2,1)S(1)} %copy-done.8) | data formatting | bytes 196608 | tf_op args[6]
  16.1 39.4 %attention.1 = (bf16[64,192]{1,0:T(8,128)(2,1)}, bf16[64,32]{1,0:T(8,128)(2,1)}, bf16[64,32]{1,0:T(8,128)(2,1)}) custom-call(bf16[64,192]{1,0:T(8,128)(2,1)} %single_ref.1, bf16[16,256]{1,0:T(8,128)(2,1)} %broadcast_in_dim.67.embedded_ref, bf16[256,192]{1,0:T(8,128)(2,1)} %copy.28.scale_ref, bf16[256,192]{1,0:T(8,128)(2,1)} %copy.29.shift_ref, ...), custom_call_target="tpu_custom_call" | custom-call | tf_op jit(solution)/shard_map/attention/pallas_call | solution.py:601
  55.5 0.0 copy-done
  55.5 1.0 %fusion.10 = f32[64,32,128]{2,0,1:T(8,128)S(1)} fusion(bf16[32,32,128]{2,1,0:T(8,128)(2,1)S(1)} %copy-done, bf16[64,32]{1,0:T(8,128)(2,1)} %get-tuple-element.6), kind=kOutput, calls=%fused_computation.13 | convolution fusion | flops 16777216 | bytes 1314816 | tf_op jit(solution)/shard_map/ip,pqc->iqc/dot_general | solution.py:641
  56.5 1.6 %copy.37.mix_ref = f32[64,32,128]{2,1,0:T(8,128)} copy(f32[64,32,128]{2,0,1:T(8,128)S(1)} %fusion.10) | data formatting | bytes 2097152 | tf_op jit(solution)/shard_map/ip,pqc->iqc/dot_general | solution.py:641
  58.1 0.7 broadcast_in_dim.77.live_keys_ref
  58.8 0.0 copy-start.9
  58.8 10.0 %transition.1 = bf16[64,64,128]{2,1,0:T(8,128)(2,1)} custom-call(f32[64]{0:T(128)} %get-tuple-element.13.live_ref, bf16[64,64,128]{2,1,0:T(8,128)(2,1)} %pair_ref.1, f32[64,32,128]{2,1,0:T(8,128)} %copy.37.mix_ref, bf16[64,32]{1,0:T(8,128)(2,1)} %get-tuple-element.7.right_ref, f32[64,128]{1,0:T(8,128)} %broadcast_in_dim.77.live_keys_ref, f32[1,128]{1,0:T(1,128)} %bitcast.23, ...), custom_call_target="tpu_custom_call" | custom-call | tf_op jit(solution)/shard_map/transition/pallas_call | solution.py:645
  68.8 0.0 copy-done.9
  68.8 0.6 copy.44
  (5 shorter events, 0.1 us)
Async XLA Ops:
  0.6 54.9 %copy-start = (bf16[32,32,128]{2,1,0:T(8,128)(2,1)S(1)}, bf16[32,32,128]{2,1,0:T(8,128)(2,1)}, u32[]{:S(2)}) copy-start(bf16[32,32,128]{2,1,0:T(8,128)(2,1)} %param.41) | copy-start | bytes 786436
  0.6 4.7 %copy-start.1 = (bf16[64,64,128]{2,1,0:T(8,128)(2,1)S(1)}, bf16[64,64,128]{2,1,0:T(8,128)(2,1)}, u32[]{:S(2)}) copy-start(bf16[64,64,128]{2,1,0:T(8,128)(2,1)} %pair_ref.1) | copy-start | bytes 3145732
  0.7 4.7 %copy-start.12 = (f32[2,12]{1,0:T(2,128)S(1)}, f32[2,12]{1,0:T(2,128)}, u32[]{:S(2)}) copy-start(f32[2,12]{1,0:T(2,128)} %param.37) | copy-start | bytes 292
  0.7 4.7 %copy-start.14 = (f32[128]{0:T(128)S(1)}, f32[128]{0:T(128)}, u32[]{:S(2)}) copy-start(f32[128]{0:T(128)} %param.35) | copy-start | bytes 1540
  0.7 4.7 %copy-start.13 = (bf16[128,12]{0,1:T(8,128)(2,1)S(1)}, bf16[128,12]{0,1:T(8,128)(2,1)}, u32[]{:S(2)}) copy-start(bf16[128,12]{0,1:T(8,128)(2,1)} %param.36) | copy-start | bytes 9220
  6.7 2.3 %copy-start.2 = (bf16[768,192]{0,1:T(8,128)(2,1)S(1)}, bf16[768,192]{0,1:T(8,128)(2,1)}, u32[]{:S(2)}) copy-start(bf16[768,192]{0,1:T(8,128)(2,1)} %param.30) | copy-start | bytes 884740
  6.7 3.2 %copy-start.3 = (bf16[768,192]{0,1:T(8,128)(2,1)S(1)}, bf16[768,192]{0,1:T(8,128)(2,1)}, u32[]{:S(2)}) copy-start(bf16[768,192]{0,1:T(8,128)(2,1)} %param.31) | copy-start | bytes 884740
  6.7 4.1 %copy-start.4 = (bf16[768,192]{0,1:T(8,128)(2,1)S(1)}, bf16[768,192]{0,1:T(8,128)(2,1)}, u32[]{:S(2)}) copy-start(bf16[768,192]{0,1:T(8,128)(2,1)} %param.32) | copy-start | bytes 884740
  7.5 4.2 %copy-start.5 = (bf16[768,192]{0,1:T(8,128)(2,1)S(1)}, bf16[768,192]{0,1:T(8,128)(2,1)}, u32[]{:S(2)}) copy-start(bf16[768,192]{0,1:T(8,128)(2,1)} %param.33) | copy-start | bytes 884740
  9.8 2.8 %copy-start.6 = (bf16[768,192]{0,1:T(8,128)(2,1)S(1)}, bf16[768,192]{0,1:T(8,128)(2,1)}, u32[]{:S(2)}) copy-start(bf16[768,192]{0,1:T(8,128)(2,1)} %param.34) | copy-start | bytes 884740
  10.8 2.8 %copy-start.10 = (f32[192,32]{0,1:T(8,128)S(1)}, f32[192,32]{0,1:T(8,128)}, u32[]{:S(2)}) copy-start(f32[192,32]{0,1:T(8,128)} %param.39) | copy-start | bytes 73732
  10.8 2.9 %copy-start.11 = (f32[192,32]{0,1:T(8,128)S(1)}, f32[192,32]{0,1:T(8,128)}, u32[]{:S(2)}) copy-start(f32[192,32]{0,1:T(8,128)} %param.40) | copy-start | bytes 73732
  11.7 2.9 %copy-start.7 = (bf16[256,192]{0,1:T(8,128)(2,1)S(1)}, bf16[256,192]{0,1:T(8,128)(2,1)}, u32[]{:S(2)}) copy-start(bf16[256,192]{0,1:T(8,128)(2,1)} %param.28) | copy-start | bytes 294916
  11.7 3.6 %copy-start.8 = (bf16[256,192]{0,1:T(8,128)(2,1)S(1)}, bf16[256,192]{0,1:T(8,128)(2,1)}, u32[]{:S(2)}) copy-start(bf16[256,192]{0,1:T(8,128)(2,1)} %param.29) | copy-start | bytes 294916
  58.8 10.0 %copy-start.9 = (bf16[64,192]{1,0:T(8,128)(2,1)S(1)}, bf16[64,192]{1,0:T(8,128)(2,1)}, u32[]{:S(2)}) copy-start(bf16[64,192]{1,0:T(8,128)(2,1)} %get-tuple-element.24) | copy-start | bytes 73732

commit v2 on v1

--- a/solution.py
+++ b/solution.py
@@ -188,6 +188,16 @@
 MESH_ID = pl.DeviceIdType.MESH
 
 
+def transposed_dot(left, right, precision=None):
+    return lax.dot_general(
+        left,
+        right,
+        (((1,), (1,)), ((), ())),
+        precision=precision,
+        preferred_element_type=jnp.float32,
+    )
+
+
 def attention_kernel(
     row_count,
     col_count,
@@ -196,17 +206,34 @@
     embedded_ref,
     scale_ref,
     shift_ref,
+    chain_ref,
+    live_ref,
+    pair_gain_ref,
+    bias_w_ref,
+    chain_bias_ref,
+    gain_ref,
+    left_w_ref,
+    right_w_ref,
+    pair_hbm,
+    query_w_hbm,
+    key_w_hbm,
+    value_w_hbm,
+    gate_w_hbm,
+    out_w_hbm,
+    outer_w_hbm,
+    single_out_ref,
+    mix_ref,
+    right_ref,
+    pair_ref,
     query_w_ref,
     key_w_ref,
     value_w_ref,
     gate_w_ref,
     out_w_ref,
-    bias_ref,
-    gain_ref,
-    factors_ref,
-    single_out_ref,
-    left_ref,
-    right_ref,
+    outer_w_ref,
+    outer_wide,
+    outer_flat,
+    packed,
     singles,
     mods,
     biases,
@@ -214,6 +241,7 @@
     gates,
     left_parts,
     right_parts,
+    load_sem,
     col_send,
     col_recv,
     row_send,
@@ -224,9 +252,12 @@
     row_place = lax.axis_index("row")
     col_place = lax.axis_index("col")
     rows, width = single_ref.shape
-    model_width = query_w_ref.shape[0]
-    factor = left_ref.shape[1]
+    half = rows // 2
+    model_width = query_w_ref.shape[1]
+    factor = left_w_ref.shape[0]
     head_count = width // head_size
+    all_heads = chain_bias_ref.shape[1]
+    channels = pair_ref.shape[2]
 
     def col_peer(step):
         return {"col": lax.rem(col_place + step, col_count)}
@@ -243,6 +274,21 @@
             device_id=device,
             device_id_type=MESH_ID,
         )
+
+    loads = [
+        pltpu.make_async_copy(source, target, load_sem.at[place])
+        for place, (source, target) in enumerate(
+            (
+                (pair_hbm, pair_ref),
+                (key_w_hbm, key_w_ref),
+                (value_w_hbm, value_w_ref),
+                (query_w_hbm, query_w_ref),
+                (gate_w_hbm, gate_w_ref),
+                (out_w_hbm, out_w_ref),
+                (outer_w_hbm, outer_w_ref),
+            )
+        )
+    ]
 
     barrier = pltpu.get_barrier_semaphore()
     for row_step in range(row_count):
@@ -254,11 +300,11 @@
                     device_id=row_peer(row_step) | col_peer(col_step),
                     device_id_type=MESH_ID,
                 )
-    embedded = embedded_ref[...]
-    mod_scale = jnp.dot(embedded, scale_ref[...], preferred_element_type=jnp.float32)
-    mod_shift = jnp.dot(embedded, shift_ref[...], preferred_element_type=jnp.float32)
-    mods[col_place, 0] = mod_scale[:8]
-    mods[col_place, 1] = mod_shift[:8]
+    for each in loads:
+        each.start()
+    embedded = jnp.broadcast_to(embedded_ref[...], (16, embedded_ref.shape[1])).astype(jnp.bfloat16)
+    mods[col_place, 0] = transposed_dot(embedded, scale_ref[...])[:8]
+    mods[col_place, 1] = transposed_dot(embedded, shift_ref[...])[:8]
     singles[col_place] = single_ref[...]
     pl.semaphore_wait(barrier, row_count * col_count - 1)
 
@@ -286,7 +332,7 @@
         )
         bias_copies.append(
             copy(
-                bias_ref.at[lax.rem(col_place + step, col_count)],
+                packed.at[lax.rem(col_place + step, col_count)],
                 biases.at[col_place],
                 col_send.at[2, step],
                 col_recv.at[2, step],
@@ -295,9 +341,52 @@
         )
     for each in first:
         each.start()
+    wide = row_count * rows
+    spot = lax.broadcasted_iota(jnp.int32, (rows, wide), 1)
+    item = lax.broadcasted_iota(jnp.int32, (rows, wide), 0)
+    slot = lax.broadcasted_iota(jnp.int32, (rows, 2 * rows), 1)
+    slot = jnp.where(slot >= rows, slot - rows, slot)
+    entry = lax.broadcasted_iota(jnp.int32, (rows, 2 * rows), 0)
+
+    def column(row_vector, place):
+        picked = jnp.where(spot == item + place * rows, row_vector, 0.0)
+        return jnp.sum(picked, axis=1, keepdims=True)
+
+    def twice(column_vector):
+        return jnp.sum(jnp.where(slot == entry, column_vector, 0.0), axis=0, keepdims=True)
+
+    chain_all = chain_ref[...].astype(jnp.float32)
+    live_all = live_ref[...].astype(jnp.float32)
+    live_column = column(live_all, col_place)
+    chain_query = column(chain_all, row_place)
+    in_first = lax.broadcasted_iota(jnp.int32, (half, 2 * rows), 1) < rows
+    chain_packed = jnp.where(in_first, chain_query[:half], chain_query[half:])
+    same = chain_packed == twice(column(chain_all, col_place))
+    live_term = jnp.where(twice(live_column) == 1.0, 0.0, MASKED)
+    loads[0].wait()
+    pair_gain = pair_gain_ref[...]
+    bias_w = bias_w_ref[...]
+
+    def score_bias(place, carry):
+        tile = jnp.concatenate([pair_ref[place], pair_ref[place + half]], axis=0)
+        normed = channel_norm(tile.astype(jnp.float32), pair_gain).astype(jnp.bfloat16)
+        found = transposed_dot(bias_w, normed)
+        for head in range(all_heads):
+            packed[
+                head // head_count, pl.ds((head % head_count) * half + place, 1), :
+            ] = found[head : head + 1]
+        return carry
+
+    lax.fori_loop(0, half, score_bias, 0, unroll=4)
+    for head in range(all_heads):
+        span = pl.ds((head % head_count) * half, half)
+        term = jnp.where(
+            same, chain_bias_ref[0:1, head : head + 1], chain_bias_ref[1:2, head : head + 1]
+        )
+        packed[head // head_count, span, :] = packed[head // head_count, span, :] + term + live_term
     for each in bias_copies:
         each.start()
-    biases[col_place] = bias_ref[col_place]
+    biases[col_place] = packed[col_place]
     for each in first:
         each.wait()
 
@@ -309,19 +398,17 @@
         squares = squares + jnp.sum(piece * piece, axis=1, keepdims=True)
     mean = total / model_width
     inv = lax.rsqrt(squares / model_width - mean * mean + EPSILON)
-    query = jnp.zeros((rows, width), jnp.float32)
-    key = jnp.zeros((rows, width), jnp.float32)
-    value = jnp.zeros((rows, width), jnp.float32)
-    gate = jnp.zeros((rows, width), jnp.float32)
-    for block in range(col_count):
-        piece = singles[block].astype(jnp.float32)
-        normed = (piece - mean) * inv * (1.0 + mods[block, 0, 0:1]) + mods[block, 1, 0:1]
-        normed = normed.astype(jnp.bfloat16)
-        span = pl.ds(block * width, width)
-        key += jnp.dot(normed, key_w_ref[span, :], preferred_element_type=jnp.float32)
-        value += jnp.dot(normed, value_w_ref[span, :], preferred_element_type=jnp.float32)
-        query += jnp.dot(normed, query_w_ref[span, :], preferred_element_type=jnp.float32)
-        gate += jnp.dot(normed, gate_w_ref[span, :], preferred_element_type=jnp.float32)
+    gathered = jnp.concatenate(
+        [singles[block].astype(jnp.float32) for block in range(col_count)], axis=1
+    )
+    mod_scale = jnp.concatenate([mods[block, 0, 0:1] for block in range(col_count)], axis=1)
+    mod_shift = jnp.concatenate([mods[block, 1, 0:1] for block in range(col_count)], axis=1)
+    normed = (gathered - mean) * inv * (1.0 + mod_scale) + mod_shift
+    normed = normed.astype(jnp.bfloat16)
+    loads[1].wait()
+    loads[2].wait()
+    key = transposed_dot(normed, key_w_ref[...])
+    value = transposed_dot(normed, value_w_ref[...])
     keys_values[row_place, 0] = key.astype(jnp.bfloat16)
     keys_values[row_place, 1] = value.astype(jnp.bfloat16)
     second = [
@@ -336,6 +423,10 @@
     ]
     for each in second:
         each.start()
+    loads[3].wait()
+    loads[4].wait()
+    query = transposed_dot(normed, query_w_ref[...])
+    gate = transposed_dot(normed, gate_w_ref[...])
     opened = jax.nn.sigmoid(gate.astype(jnp.bfloat16).astype(jnp.float32))
     query = query.astype(jnp.bfloat16)
     lane = lax.broadcasted_iota(jnp.int32, (rows, width), 1)
@@ -345,19 +436,27 @@
     query_heads = jnp.concatenate(
         [jnp.where(mask, query, jnp.zeros_like(query)) for mask in masks], axis=0
     )
+    loads[6].wait()
+    outer_wide[...] = outer_w_ref[...].astype(jnp.float32)
+    for place in range(factor):
+        outer_flat[:, place * channels : (place + 1) * channels] = outer_wide[:, place, :].astype(
+            jnp.bfloat16
+        )
     for each in bias_copies:
         each.wait()
     for each in second:
         each.wait()
+
+    def unpack(block):
+        held = biases[block]
+        pieces = []
+        for head in range(head_count):
+            part = held[head * half : (head + 1) * half]
+            pieces += [part[:, :rows], part[:, rows:]]
+        return jnp.concatenate(pieces, axis=0)
+
     scores = [
-        lax.dot_general(
-            query_heads,
-            keys_values[block, 0],
-            (((1,), (1,)), ((), ())),
-            preferred_element_type=jnp.float32,
-        )
-        * head_size ** (-0.5)
-        + biases[block]
+        transposed_dot(query_heads, keys_values[block, 0]) * head_size ** (-0.5) + unpack(block)
         for block in range(row_count)
     ]
     top = functools.reduce(jnp.maximum, [jnp.max(s, axis=1, keepdims=True) for s in scores])
@@ -391,25 +490,27 @@
         each.start()
     for each in third:
         each.wait()
-    mixed = single_ref[...].astype(jnp.float32)
-    for block in range(col_count):
-        mixed += jnp.dot(
-            gates[block],
-            out_w_ref[pl.ds(block * width, width), :],
-            preferred_element_type=jnp.float32,
-        )
+    loads[5].wait()
+    gated = jnp.concatenate(
+        [gates[block].astype(jnp.float32) for block in range(col_count)], axis=1
+    ).astype(jnp.bfloat16)
+    mixed = single_ref[...].astype(jnp.float32) + transposed_dot(gated, out_w_ref[...])
     single_out = mixed.astype(jnp.bfloat16)
     single_out_ref[...] = single_out
     updated = single_out.astype(jnp.float32)
     gain = gain_ref[...]
     stacked = jnp.concatenate([updated * gain, jnp.broadcast_to(gain, (8, width))], axis=0)
-    products = jnp.dot(
-        stacked,
-        factors_ref[...],
-        precision=lax.Precision.HIGHEST,
-        preferred_element_type=jnp.float32,
-    )
-    place = lax.broadcasted_iota(jnp.int32, (rows, products.shape[1]), 1)
+    lanes = left_parts.shape[2]
+    factors = jnp.concatenate(
+        [
+            left_w_ref[...],
+            right_w_ref[...],
+            jnp.zeros((lanes - 2 * factor, width), jnp.float32),
+        ],
+        axis=0,
+    )
+    products = transposed_dot(stacked, factors, lax.Precision.HIGHEST)
+    place = lax.broadcasted_iota(jnp.int32, (rows, lanes), 1)
     left_parts[col_place, pl.ds(0, rows), :] = jnp.where(
         place == 2 * factor,
         jnp.sum(updated, axis=1, keepdims=True),
@@ -467,7 +568,13 @@
         out_inv = lax.rsqrt(out_square - out_mean * out_mean + EPSILON)
         return out_inv * (body_rows - out_mean * joint[rows : rows + 1])
 
-    left_ref[...] = finish(left_parts)[:, :factor].astype(jnp.bfloat16)
+    left = finish(left_parts)[:, :factor].astype(jnp.bfloat16)
+    for which in range(factor):
+        mix_ref[:, which, :] = jnp.dot(
+            left,
+            outer_flat[:, which * channels : (which + 1) * channels],
+            preferred_element_type=jnp.float32,
+        )
     for block in range(col_count):
 
         @pl.when(jnp.logical_not(diagonal & (col_place == block)))
@@ -480,7 +587,10 @@
                 row_peer(0),
             ).wait_recv()
 
-    right_ref[...] = finish(right_parts)[:, factor : 2 * factor].astype(jnp.bfloat16)
+    right = finish(right_parts).astype(jnp.bfloat16).astype(jnp.float32)
+    right = jnp.where((place >= factor) & (place < 2 * factor), right, 0.0)
+    right = jnp.where(place == 0, 1.0, right) * live_column
+    right_ref[...] = (right + pltpu.roll(right, 2 * factor, 1)).astype(jnp.bfloat16)
     for step in range(1, row_count):
         right_copies[step].wait_send()
 
@@ -494,7 +604,6 @@
     pair_ref,
     mix_ref,
     right_ref,
-    live_keys_ref,
     outer_bias_ref,
     gain_ref,
     w_in_ref,
@@ -503,21 +612,21 @@
     flat_ref,
 ):
     block_rows, key_rows, channels = pair_ref.shape
-    start = pl.program_id(0) * block_rows
+    start = lax.axis_index("row") * key_rows + pl.program_id(0) * block_rows
     right = right_ref[...]
-    right_twice = jnp.concatenate([right, right], axis=1)
-    live_keys = live_keys_ref[...]
-    outer_bias = outer_bias_ref[...]
+    factor = mix_ref.shape[1]
+    top = lax.broadcasted_iota(jnp.int32, (factor, channels), 0)
+    bias_rows = jnp.where(top == 0, outer_bias_ref[...], 0.0)
     for place in range(block_rows):
-        mix = mix_ref[place]
-        high = mix.astype(jnp.bfloat16)
-        low = (mix - high.astype(jnp.float32)).astype(jnp.bfloat16)
+        terms = jnp.concatenate([bias_rows, mix_ref[place]], axis=0)
+        high = terms.astype(jnp.bfloat16)
+        low = (terms - high.astype(jnp.float32)).astype(jnp.bfloat16)
         outer = jnp.dot(
-            right_twice,
+            right,
             jnp.concatenate([high, low], axis=0),
             preferred_element_type=jnp.float32,
         )
-        outer = (outer + outer_bias) * (live_keys * live_ref[start + place])
+        outer = outer * live_ref[start + place].astype(jnp.float32)
         flat_ref[pl.ds(place * key_rows, key_rows), :] = pair_ref[place].astype(jnp.float32) + outer
     flat = flat_ref[...]
     normed = channel_norm(flat, gain_ref[...]).astype(jnp.bfloat16)
@@ -573,48 +682,42 @@
     local_heads = head_count // col_count
     factor = w_left.shape[1]
     channels = pair.shape[2]
-    query_start = lax.axis_index("row") * rows
-    key_start = lax.axis_index("col") * rows
-    chain_query = lax.dynamic_slice_in_dim(chain, query_start, rows, 0)
-    chain_key = lax.dynamic_slice_in_dim(chain, key_start, rows, 0)
-    live_query = lax.dynamic_slice_in_dim(live, query_start, rows, 0).astype(jnp.float32)
-    live_keys = lax.dynamic_slice_in_dim(live, key_start, rows, 0)
     embedded = time_embed(step_index, time_scale.shape[0]).astype(jnp.bfloat16)
-    embedded = jnp.broadcast_to(embedded[None], (16, embedded.shape[0]))
-    pair_normed = channel_norm(pair.astype(jnp.float32), pair_gain).astype(jnp.bfloat16)
-    bias_terms = jnp.einsum(
-        "qkc,ch->hqk", pair_normed, bias_weight, preferred_element_type=jnp.float32
-    )
-    same_chain = chain_query[:, None] == chain_key[None, :]
-    chain_terms = jnp.where(
-        same_chain[None], chain_bias[0][:, None, None], chain_bias[1][:, None, None]
-    )
-    live_terms = jnp.where(live_keys == 1, 0.0, MASKED).astype(jnp.float32)
-    bias_terms = bias_terms + chain_terms + live_terms[None, None, :]
-    bias_terms = bias_terms.reshape(col_count, local_heads * rows, rows)
-    lanes = 128 * pl.cdiv(2 * factor + 2, 128)
-    factors = jnp.concatenate(
-        [w_left, w_right, jnp.zeros((width, lanes - 2 * factor), jnp.float32)], axis=1
-    )
+    lanes = 4 * factor
+    tile_heads = 16 * pl.cdiv(head_count, 16)
+    bias_w = jnp.pad(bias_weight.T, ((0, tile_heads - head_count), (0, 0)))
     vmem = pl.BlockSpec(memory_space=pltpu.VMEM)
     bf16, f32 = jnp.bfloat16, jnp.float32
-    single_out, left, right = pl.pallas_call(
+    hbm = pl.BlockSpec(memory_space=pl.ANY)
+    weight = pltpu.VMEM((width, model_width), bf16)
+    single_out, mix, right = pl.pallas_call(
         functools.partial(attention_kernel, row_count, col_count, head_size),
         out_shape=(
             jax.ShapeDtypeStruct((rows, width), bf16),
-            jax.ShapeDtypeStruct((rows, factor), bf16),
-            jax.ShapeDtypeStruct((rows, factor), bf16),
+            jax.ShapeDtypeStruct((rows, factor, channels), f32),
+            jax.ShapeDtypeStruct((rows, lanes), bf16),
         ),
-        in_specs=[vmem] * 12,
+        in_specs=[vmem] * 12 + [hbm] * 7,
         out_specs=(vmem, vmem, vmem),
         scratch_shapes=[
+            pltpu.VMEM(pair.shape, bf16),
+            weight,
+            weight,
+            weight,
+            weight,
+            weight,
+            pltpu.VMEM(w_outer.shape, bf16),
+            pltpu.VMEM(w_outer.shape, f32),
+            pltpu.VMEM((factor, factor * channels), bf16),
+            pltpu.VMEM((col_count, local_heads * rows // 2, 2 * rows), f32),
             pltpu.VMEM((col_count, rows, width), bf16),
             pltpu.VMEM((col_count, 2, 8, width), f32),
-            pltpu.VMEM((col_count, local_heads * rows, rows), f32),
+            pltpu.VMEM((col_count, local_heads * rows // 2, 2 * rows), f32),
             pltpu.VMEM((row_count, 2, rows, width), bf16),
             pltpu.VMEM((col_count, rows, width), bf16),
             pltpu.VMEM((col_count, rows + 8, lanes), f32),
             pltpu.VMEM((col_count, rows + 8, lanes), f32),
+            pltpu.SemaphoreType.DMA((7,)),
             pltpu.SemaphoreType.DMA((5, col_count)),
             pltpu.SemaphoreType.DMA((5, col_count)),
             pltpu.SemaphoreType.DMA((row_count,)),
@@ -626,20 +729,25 @@
         name="attention",
     )(
         single,
-        embedded,
-        time_scale,
-        time_shift,
-        w_query,
-        w_key,
-        w_value,
-        w_gate,
-        w_out,
-        bias_terms,
+        embedded[None].astype(f32),
+        time_scale.T,
+        time_shift.T,
+        chain[None],
+        live[None],
+        pair_gain[None],
+        bias_w,
+        chain_bias,
         outer_gain[None],
-        factors,
-    )
-    left_mix = jnp.einsum("ip,pqc->iqc", left, w_outer, preferred_element_type=jnp.float32)
-    live_lanes = jnp.broadcast_to(live_keys.astype(jnp.float32)[:, None], (rows, channels))
+        w_left.T,
+        w_right.T,
+        pair,
+        w_query.T,
+        w_key.T,
+        w_value.T,
+        w_gate.T,
+        w_out.T,
+        w_outer,
+    )
     block = math.gcd(rows, 8)
     hidden = w_down.shape[0]
     pair_out = pl.pallas_call(
@@ -650,8 +758,7 @@
             pl.BlockSpec(memory_space=pltpu.SMEM),
             pl.BlockSpec((block, rows, channels), lambda i: (i, 0, 0)),
             pl.BlockSpec((block, factor, channels), lambda i: (i, 0, 0)),
-            pl.BlockSpec((rows, factor), lambda i: (0, 0)),
-            pl.BlockSpec((rows, channels), lambda i: (0, 0)),
+            pl.BlockSpec((rows, lanes), lambda i: (0, 0)),
             pl.BlockSpec((1, channels), lambda i: (0, 0)),
             pl.BlockSpec((1, channels), lambda i: (0, 0)),
             pl.BlockSpec((channels, 2 * hidden), lambda i: (0, 0)),
@@ -661,11 +768,10 @@
         scratch_shapes=[pltpu.VMEM((block * rows, channels), f32)],
         name="transition",
     )(
-        live_query,
+        live,
         pair,
-        left_mix,
+        mix,
         right,
-        live_lanes,
         outer_bias[None],
         trans_gain[None],
         w_in,

time: 69.8 us -> 49.6 us (0.71)
  local copies, waits for them, and re-layouts: 10.8 us -> 1.27 us
  other arithmetic: 5.42 us -> 0.62 us
  Pallas kernels: 49.4 us -> 46.1 us
  matrix products: 2.27 us -> 0 us
    unnamed x40 -> x5, local copies, waits for them, and re-layouts: 6.99 us -> 0.67 us
    pallas_call x1, Pallas kernels: 39.4 us -> 36.4 us  [fast_body(): pl.pallas_call(functools.partial(attention_kernel, row_count, col_count,...]
    reduce_sum x1 -> x0, other arithmetic: 2.38 us -> none  [channel_norm(): row_mean = jnp.mean(values, axis=-1, keepdims=True)]
    dot_general x2 -> x0, matrix products: 2.27 us -> none  [the longest x1 1.28 us: fast_body(): jnp.einsum('qkc,ch->hqk', pair_normed, bias_weight, preferred_element_typ...]
    dot_general x1 -> x0, local copies, waits for them, and re-layouts: 1.59 us -> none  [fast_body(): jnp.einsum('ip,pqc->iqc', left, w_outer, preferred_element_type=jnp.float32)]
    broadcast_in_dim x4 -> x0, local copies, waits for them, and re-layouts: 1.3 us -> none  [the longest x1 0.69 us: fast_body(): jnp.broadcast_to(live_keys.astype(jnp.float32)[:, None], (rows, channels))]
    add x1 -> x0, local copies, waits for them, and re-layouts: 0.87 us -> none  [fast_body(): bias_terms = bias_terms + chain_terms + live_terms[None, None, :]]
    convert_element_type x1, other arithmetic: 1.41 us -> 0.57 us  [fast_body(): embedded[None].astype(f32)]
where the time goes in v2:
time: 49.6 us; the launch traced here: 49.3 us
  Pallas kernels  46.1 us (93%)
  between operations  1.31 us (3%)
  local copies, waits for them, and re-layouts  1.27 us (3%)
  other arithmetic  0.62 us (1%)
    pallas_call x1, Pallas kernels, fast_body(): pl.pallas_call(functools.partial(attention_kernel, row_count, col_count,...  36.4 us
    pallas_call x1, Pallas kernels, fast_body(): pl.pallas_call(pair_kernel, grid=(rows // block,), out_shape=jax.ShapeDty...  9.7 us

profile of v2, /device:TPU:0, one launch (start us, length us, event | category | flops | bytes accessed | tf_op | source)
XLA Modules:
  0.0 49.3 jit_solution(16920271596350767084)
XLA Ops:
  1.3 0.0 copy-start.1
  1.3 0.6 %maximum_convert_fusion.embedded_ref = f32[1,256]{1,0:T(1,128)} fusion(bf16[1,128]{1,0:T(2,128)(2,1)S(1)} %get-tuple-element.8, bf16[1,128]{1,0:T(2,128)(2,1)S(1)} %get-tuple-element.9), kind=kLoop, calls=%fused_computation | loop fusion | flops 1024 | bytes 1536 | tf_op jit(solution)/shard_map/convert_element_type | solution.py:732
  1.9 0.1 copy-done.1
  2.0 0.6 %pad.4.bias_w_ref = bf16[16,128]{1,0:T(8,128)(2,1)} pad(bf16[12,128]{1,0:T(8,128)(2,1)S(1)} %bitcast.31, bf16[]{:T(256)} %constant.7.clone.1), padding=0_4x0_0 | pad | bytes 7170 | tf_op jit(solution)/shard_map/jit(_pad)/pad | solution.py:688
  2.6 36.4 %attention.1 = (bf16[64,192]{1,0:T(8,128)(2,1)}, f32[64,32,128]{2,1,0:T(8,128)}, bf16[64,128]{1,0:T(8,128)(2,1)}) custom-call(bf16[64,192]{1,0:T(8,128)(2,1)} %single_ref.1, f32[1,256]{1,0:T(1,128)} %maximum_convert_fusion.embedded_ref, bf16[192,256]{1,0:T(8,128)(2,1)} %bitcast.26, bf16[192,256]{1,0:T(8,128)(2,1)} %bitcast.27, s32[1,256]{1,0:T(1,128)} %bitcast.32, ...), custom_call_target="tpu_custom_call" | custom-call | tf_op jit(solution)/shard_map/attention/pallas_call | solution.py:693
  38.9 0.0 copy-start
  38.9 9.7 %transition.1 = bf16[64,64,128]{2,1,0:T(8,128)(2,1)} custom-call(s32[256]{0:T(256)} %live_ref.1, bf16[64,64,128]{2,1,0:T(8,128)(2,1)} %pair_ref.1, f32[64,32,128]{2,1,0:T(8,128)} %get-tuple-element.6.mix_ref, bf16[64,128]{1,0:T(8,128)(2,1)} %get-tuple-element.7.right_ref, f32[1,128]{1,0:T(1,128)} %bitcast.35, f32[1,128]{1,0:T(1,128)} %bitcast.36, ...), custom_call_target="tpu_custom_call" | custom-call | tf_op jit(solution)/shard_map/transition/pallas_call | solution.py:753
  48.6 0.0 copy-done
  48.6 0.6 %copy.27 = bf16[64,192]{1,0:T(8,128)(2,1)} copy(bf16[64,192]{1,0:T(8,128)(2,1)S(1)} %copy-done) | data formatting | bytes 49152
  (1 shorter events, 0.0 us)
Async XLA Ops:
  1.3 0.7 %copy-start.1 = (bf16[128,12]{0,1:T(8,128)(2,1)S(1)}, bf16[128,12]{0,1:T(8,128)(2,1)}, u32[]{:S(2)}) copy-start(bf16[128,12]{0,1:T(8,128)(2,1)} %param.36) | copy-start | bytes 9220
  38.9 9.7 %copy-start = (bf16[64,192]{1,0:T(8,128)(2,1)S(1)}, bf16[64,192]{1,0:T(8,128)(2,1)}, u32[]{:S(2)}) copy-start(bf16[64,192]{1,0:T(8,128)(2,1)} %get-tuple-element.12) | copy-start | bytes 73732

commit v3 on v2

--- a/solution.py
+++ b/solution.py
@@ -198,6 +198,27 @@
     )
 
 
+def pack(values):
+    rows, width = values.shape
+    whole = width - width % 128
+    if rows % 32 or 2 * (width - whole) != 128:
+        return values
+    half = rows // 2
+    rest = jnp.concatenate([values[:half, whole:], values[half:, whole:]], axis=1)
+    columns = [values[:, place : place + 128] for place in range(0, whole, 128)]
+    return jnp.concatenate(columns + [rest], axis=0)
+
+
+def unpack(held, rows, width):
+    whole = width - width % 128
+    if held.shape == (rows, width):
+        return held
+    rest = held[(whole // 128) * rows :]
+    rest = jnp.concatenate([rest[:, :64], rest[:, 64:]], axis=0)
+    columns = [held[place * rows : (place + 1) * rows] for place in range(whole // 128)]
+    return jnp.concatenate(columns + [rest], axis=1)
+
+
 def attention_kernel(
     row_count,
     col_count,
@@ -241,6 +262,7 @@
     gates,
     left_parts,
     right_parts,
+    own_right,
     load_sem,
     col_send,
     col_recv,
@@ -303,9 +325,11 @@
     for each in loads:
         each.start()
     embedded = jnp.broadcast_to(embedded_ref[...], (16, embedded_ref.shape[1])).astype(jnp.bfloat16)
-    mods[col_place, 0] = transposed_dot(embedded, scale_ref[...])[:8]
-    mods[col_place, 1] = transposed_dot(embedded, shift_ref[...])[:8]
-    singles[col_place] = single_ref[...]
+    mod_scale = transposed_dot(embedded, scale_ref[...])[:8]
+    mod_shift = transposed_dot(embedded, shift_ref[...])[:8]
+    mod_row = lax.broadcasted_iota(jnp.int32, mod_scale.shape, 0)
+    mods[col_place] = jnp.where(mod_row == 0, mod_scale, mod_shift)
+    singles[col_place] = pack(single_ref[...].astype(jnp.float32)).astype(jnp.bfloat16)
     pl.semaphore_wait(barrier, row_count * col_count - 1)
 
     first = []
@@ -314,7 +338,7 @@
         peer = col_peer(step)
         first.append(
             copy(
-                single_ref,
+                singles.at[col_place],
                 singles.at[col_place],
                 col_send.at[0, step],
                 col_recv.at[0, step],
@@ -390,19 +414,16 @@
     for each in first:
         each.wait()
 
-    total = jnp.zeros((rows, 1), jnp.float32)
-    squares = jnp.zeros((rows, 1), jnp.float32)
-    for block in range(col_count):
-        piece = singles[block].astype(jnp.float32)
-        total = total + jnp.sum(piece, axis=1, keepdims=True)
-        squares = squares + jnp.sum(piece * piece, axis=1, keepdims=True)
+    gathered = jnp.concatenate(
+        [unpack(singles[block].astype(jnp.float32), rows, width) for block in range(col_count)],
+        axis=1,
+    )
+    mod_scale = jnp.concatenate([mods[block, 0:1] for block in range(col_count)], axis=1)
+    mod_shift = jnp.concatenate([mods[block, 1:2] for block in range(col_count)], axis=1)
+    total = jnp.sum(gathered, axis=1, keepdims=True)
+    squares = jnp.sum(gathered * gathered, axis=1, keepdims=True)
     mean = total / model_width
     inv = lax.rsqrt(squares / model_width - mean * mean + EPSILON)
-    gathered = jnp.concatenate(
-        [singles[block].astype(jnp.float32) for block in range(col_count)], axis=1
-    )
-    mod_scale = jnp.concatenate([mods[block, 0, 0:1] for block in range(col_count)], axis=1)
-    mod_shift = jnp.concatenate([mods[block, 1, 0:1] for block in range(col_count)], axis=1)
     normed = (gathered - mean) * inv * (1.0 + mod_scale) + mod_shift
     normed = normed.astype(jnp.bfloat16)
     loads[1].wait()
@@ -447,7 +468,7 @@
     for each in second:
         each.wait()
 
-    def unpack(block):
+    def unpack_bias(block):
         held = biases[block]
         pieces = []
         for head in range(head_count):
@@ -456,7 +477,7 @@
         return jnp.concatenate(pieces, axis=0)
 
     scores = [
-        transposed_dot(query_heads, keys_values[block, 0]) * head_size ** (-0.5) + unpack(block)
+        transposed_dot(query_heads, keys_values[block, 0]) * head_size ** (-0.5) + unpack_bias(block)
         for block in range(row_count)
     ]
     top = functools.reduce(jnp.maximum, [jnp.max(s, axis=1, keepdims=True) for s in scores])
@@ -475,7 +496,7 @@
         jnp.where(masks[head], summed[head * rows : (head + 1) * rows], 0.0)
         for head in range(head_count)
     )
-    gates[col_place] = (opened * attended).astype(jnp.bfloat16)
+    gates[col_place] = pack(opened * attended).astype(jnp.bfloat16)
     third = [
         copy(
             gates.at[col_place],
@@ -492,35 +513,37 @@
         each.wait()
     loads[5].wait()
     gated = jnp.concatenate(
-        [gates[block].astype(jnp.float32) for block in range(col_count)], axis=1
+        [unpack(gates[block].astype(jnp.float32), rows, width) for block in range(col_count)],
+        axis=1,
     ).astype(jnp.bfloat16)
     mixed = single_ref[...].astype(jnp.float32) + transposed_dot(gated, out_w_ref[...])
     single_out = mixed.astype(jnp.bfloat16)
     single_out_ref[...] = single_out
     updated = single_out.astype(jnp.float32)
     gain = gain_ref[...]
-    stacked = jnp.concatenate([updated * gain, jnp.broadcast_to(gain, (8, width))], axis=0)
-    lanes = left_parts.shape[2]
-    factors = jnp.concatenate(
+    precise = lax.Precision.HIGHEST
+    factors = jnp.concatenate([left_w_ref[...], right_w_ref[...]], axis=0)
+    products = transposed_dot(factors, updated * gain, precise)
+    ones = jnp.ones((8, width), jnp.float32)
+    totals = jnp.concatenate(
         [
-            left_w_ref[...],
-            right_w_ref[...],
-            jnp.zeros((lanes - 2 * factor, width), jnp.float32),
+            transposed_dot(ones, updated, precise),
+            transposed_dot(ones, updated * updated, precise),
         ],
-        axis=0,
-    )
-    products = transposed_dot(stacked, factors, lax.Precision.HIGHEST)
-    place = lax.broadcasted_iota(jnp.int32, (rows, lanes), 1)
-    left_parts[col_place, pl.ds(0, rows), :] = jnp.where(
-        place == 2 * factor,
-        jnp.sum(updated, axis=1, keepdims=True),
-        jnp.where(
-            place == 2 * factor + 1,
-            jnp.sum(updated * updated, axis=1, keepdims=True),
-            products[:rows],
-        ),
-    )
-    left_parts[col_place, pl.ds(rows, 8), :] = products[rows:]
+        axis=1,
+    )
+    weight_sums = transposed_dot(jnp.broadcast_to(gain, (8, width)), factors, precise)
+    weight_sums = jnp.concatenate([weight_sums, jnp.zeros_like(totals[:, 2 * factor :])], axis=1)
+    stat_row = lax.broadcasted_iota(jnp.int32, totals.shape, 0)
+    statistics = jnp.where(stat_row == 0, totals, weight_sums)
+    part = factor // 2
+    for parts, start in ((left_parts, 0), (own_right, factor)):
+        sides = [products[start : start + part], products[start + part : start + factor]]
+        joined = jnp.concatenate([jnp.concatenate(sides, axis=1), statistics], axis=0)
+        if parts is left_parts:
+            parts[col_place] = joined
+        else:
+            parts[...] = joined
     fourth = [
         copy(
             left_parts.at[col_place],
@@ -533,7 +556,7 @@
     ]
     right_copies = [
         copy(
-            left_parts.at[col_place],
+            own_right,
             right_parts.at[col_place],
             right_send.at[step],
             right_recv.at[col_place],
@@ -553,22 +576,27 @@
 
     @pl.when(diagonal)
     def _():
-        right_parts[col_place] = left_parts[col_place]
+        right_parts[col_place] = own_right[...]
 
     for each in fourth:
         each.wait()
 
-    def finish(parts):
+    which_factor = lax.broadcasted_iota(jnp.int32, (factor, 2 * rows), 0)
+    which_lane = lax.broadcasted_iota(jnp.int32, (factor, 2 * rows), 1)
+
+    def finish(parts, start):
         joint = parts[0]
         for block in range(1, col_count):
             joint = joint + parts[block]
-        body_rows = joint[:rows]
-        out_mean = body_rows[:, 2 * factor : 2 * factor + 1] / model_width
-        out_square = body_rows[:, 2 * factor + 1 : 2 * factor + 2] / model_width
+        out_mean = joint[part : part + 1, :rows] / model_width
+        out_square = joint[part : part + 1, rows:] / model_width
         out_inv = lax.rsqrt(out_square - out_mean * out_mean + EPSILON)
-        return out_inv * (body_rows - out_mean * joint[rows : rows + 1])
-
-    left = finish(left_parts)[:, :factor].astype(jnp.bfloat16)
+        picked = jnp.where(which_lane == which_factor + start, joint[part + 1 : part + 2], 0.0)
+        sums = jnp.sum(picked, axis=1, keepdims=True)
+        body_rows = jnp.concatenate([joint[:part, :rows], joint[:part, rows:]], axis=0)
+        return out_inv * (body_rows - out_mean * sums)
+
+    left = finish(left_parts, 0).T.astype(jnp.bfloat16)
     for which in range(factor):
         mix_ref[:, which, :] = jnp.dot(
             left,
@@ -580,17 +608,17 @@
         @pl.when(jnp.logical_not(diagonal & (col_place == block)))
         def _():
             copy(
-                left_parts.at[block],
+                own_right,
                 right_parts.at[block],
                 right_send.at[0],
                 right_recv.at[block],
                 row_peer(0),
             ).wait_recv()
 
-    right = finish(right_parts).astype(jnp.bfloat16).astype(jnp.float32)
-    right = jnp.where((place >= factor) & (place < 2 * factor), right, 0.0)
-    right = jnp.where(place == 0, 1.0, right) * live_column
-    right_ref[...] = (right + pltpu.roll(right, 2 * factor, 1)).astype(jnp.bfloat16)
+    right = finish(right_parts, factor).astype(jnp.bfloat16).astype(jnp.float32)
+    top = jnp.where(lax.broadcasted_iota(jnp.int32, right.shape, 0) == 0, 1.0, 0.0)
+    right = jnp.concatenate([top, right, top, right], axis=0).T * live_column
+    right_ref[...] = right.astype(jnp.bfloat16)
     for step in range(1, row_count):
         right_copies[step].wait_send()
 
@@ -688,6 +716,7 @@
     bias_w = jnp.pad(bias_weight.T, ((0, tile_heads - head_count), (0, 0)))
     vmem = pl.BlockSpec(memory_space=pltpu.VMEM)
     bf16, f32 = jnp.bfloat16, jnp.float32
+    packed_shape = jax.eval_shape(pack, jax.ShapeDtypeStruct((rows, width), f32)).shape
     hbm = pl.BlockSpec(memory_space=pl.ANY)
     weight = pltpu.VMEM((width, model_width), bf16)
     single_out, mix, right = pl.pallas_call(
@@ -710,13 +739,14 @@
             pltpu.VMEM(w_outer.shape, f32),
             pltpu.VMEM((factor, factor * channels), bf16),
             pltpu.VMEM((col_count, local_heads * rows // 2, 2 * rows), f32),
-            pltpu.VMEM((col_count, rows, width), bf16),
-            pltpu.VMEM((col_count, 2, 8, width), f32),
+            pltpu.VMEM((col_count,) + packed_shape, bf16),
+            pltpu.VMEM((col_count, 8, width), f32),
             pltpu.VMEM((col_count, local_heads * rows // 2, 2 * rows), f32),
             pltpu.VMEM((row_count, 2, rows, width), bf16),
-            pltpu.VMEM((col_count, rows, width), bf16),
-            pltpu.VMEM((col_count, rows + 8, lanes), f32),
-            pltpu.VMEM((col_count, rows + 8, lanes), f32),
+            pltpu.VMEM((col_count,) + packed_shape, bf16),
+            pltpu.VMEM((col_count, factor // 2 + 8, 2 * rows), f32),
+            pltpu.VMEM((col_count, factor // 2 + 8, 2 * rows), f32),
+            pltpu.VMEM((factor // 2 + 8, 2 * rows), f32),
             pltpu.SemaphoreType.DMA((7,)),
             pltpu.SemaphoreType.DMA((5, col_count)),
             pltpu.SemaphoreType.DMA((5, col_count)),
@@ -748,7 +778,7 @@
         w_out.T,
         w_outer,
     )
-    block = math.gcd(rows, 8)
+    block = math.gcd(rows, 32)
     hidden = w_down.shape[0]
     pair_out = pl.pallas_call(
         pair_kernel,

time: 49.6 us -> 38.7 us (0.78)
  Pallas kernels: 46.1 us -> 35.3 us
    pallas_call x1, Pallas kernels: 36.4 us -> 28.1 us  [fast_body(): pl.pallas_call(functools.partial(attention_kernel, row_count, col_count,...]
    pallas_call x1, Pallas kernels: 9.7 us -> 7.14 us  [fast_body(): pl.pallas_call(pair_kernel, grid=(rows // block,), out_shape=jax.ShapeDty...]
where the time goes in v3:
time: 38.7 us; the launch traced here: 38.5 us
  Pallas kernels  35.3 us (91%)
  between operations  1.31 us (3%)
  local copies, waits for them, and re-layouts  1.27 us (3%)
  other arithmetic  0.62 us (2%)
    pallas_call x1, Pallas kernels, fast_body(): pl.pallas_call(functools.partial(attention_kernel, row_count, col_count,...  28.1 us
    pallas_call x1, Pallas kernels, fast_body(): pl.pallas_call(pair_kernel, grid=(rows // block,), out_shape=jax.ShapeDty...  7.14 us

profile of v3, /device:TPU:0, one launch (start us, length us, event | category | flops | bytes accessed | tf_op | source)
XLA Modules:
  0.0 38.5 jit_solution(1994721838195839224)
XLA Ops:
  1.3 0.0 copy-start.1
  1.3 0.6 %maximum_convert_fusion.embedded_ref = f32[1,256]{1,0:T(1,128)} fusion(bf16[1,128]{1,0:T(2,128)(2,1)S(1)} %get-tuple-element.8, bf16[1,128]{1,0:T(2,128)(2,1)S(1)} %get-tuple-element.9), kind=kLoop, calls=%fused_computation | loop fusion | flops 1024 | bytes 1536 | tf_op jit(solution)/shard_map/convert_element_type | solution.py:762
  1.9 0.1 copy-done.1
  2.0 0.6 %pad.4.bias_w_ref = bf16[16,128]{1,0:T(8,128)(2,1)} pad(bf16[12,128]{1,0:T(8,128)(2,1)S(1)} %bitcast.31, bf16[]{:T(256)} %constant.7.clone.1), padding=0_4x0_0 | pad | bytes 7170 | tf_op jit(solution)/shard_map/jit(_pad)/pad | solution.py:716
  2.6 28.1 %attention.1 = (bf16[64,192]{1,0:T(8,128)(2,1)}, f32[64,32,128]{2,1,0:T(8,128)}, bf16[64,128]{1,0:T(8,128)(2,1)}) custom-call(bf16[64,192]{1,0:T(8,128)(2,1)} %single_ref.1, f32[1,256]{1,0:T(1,128)} %maximum_convert_fusion.embedded_ref, bf16[192,256]{1,0:T(8,128)(2,1)} %bitcast.26, bf16[192,256]{1,0:T(8,128)(2,1)} %bitcast.27, s32[1,256]{1,0:T(1,128)} %bitcast.32, ...), custom_call_target="tpu_custom_call" | custom-call | tf_op jit(solution)/shard_map/attention/pallas_call | solution.py:722
  30.7 0.0 copy-start
  30.7 7.1 %transition.1 = bf16[64,64,128]{2,1,0:T(8,128)(2,1)} custom-call(s32[256]{0:T(256)} %live_ref.1, bf16[64,64,128]{2,1,0:T(8,128)(2,1)} %pair_ref.1, f32[64,32,128]{2,1,0:T(8,128)} %get-tuple-element.6.mix_ref, bf16[64,128]{1,0:T(8,128)(2,1)} %get-tuple-element.7.right_ref, f32[1,128]{1,0:T(1,128)} %bitcast.35, f32[1,128]{1,0:T(1,128)} %bitcast.36, ...), custom_call_target="tpu_custom_call" | custom-call | tf_op jit(solution)/shard_map/transition/pallas_call | solution.py:783
  37.8 0.0 copy-done
  37.8 0.6 %copy.27 = bf16[64,192]{1,0:T(8,128)(2,1)} copy(bf16[64,192]{1,0:T(8,128)(2,1)S(1)} %copy-done) | data formatting | bytes 49152
  (1 shorter events, 0.0 us)
Async XLA Ops:
  1.3 0.7 %copy-start.1 = (bf16[128,12]{0,1:T(8,128)(2,1)S(1)}, bf16[128,12]{0,1:T(8,128)(2,1)}, u32[]{:S(2)}) copy-start(bf16[128,12]{0,1:T(8,128)(2,1)} %param.36) | copy-start | bytes 9220
  30.7 7.2 %copy-start = (bf16[64,192]{1,0:T(8,128)(2,1)S(1)}, bf16[64,192]{1,0:T(8,128)(2,1)}, u32[]{:S(2)}) copy-start(bf16[64,192]{1,0:T(8,128)(2,1)} %get-tuple-element.12) | copy-start | bytes 73732

commit v4 on v3

--- a/solution.py
+++ b/solution.py
@@ -565,14 +565,15 @@
         for step in range(row_count)
     ]
     diagonal = row_place == col_place
-    for each in fourth:
-        each.start()
     for step in range(1, row_count):
         right_copies[step].start()
 
     @pl.when(jnp.logical_not(diagonal))
     def _():
         right_copies[0].start()
+
+    for each in fourth:
+        each.start()
 
     @pl.when(diagonal)
     def _():
@@ -712,8 +713,6 @@
     channels = pair.shape[2]
     embedded = time_embed(step_index, time_scale.shape[0]).astype(jnp.bfloat16)
     lanes = 4 * factor
-    tile_heads = 16 * pl.cdiv(head_count, 16)
-    bias_w = jnp.pad(bias_weight.T, ((0, tile_heads - head_count), (0, 0)))
     vmem = pl.BlockSpec(memory_space=pltpu.VMEM)
     bf16, f32 = jnp.bfloat16, jnp.float32
     packed_shape = jax.eval_shape(pack, jax.ShapeDtypeStruct((rows, width), f32)).shape
@@ -765,7 +764,7 @@
         chain[None],
         live[None],
         pair_gain[None],
-        bias_w,
+        bias_weight.T,
         chain_bias,
         outer_gain[None],
         w_left.T,

time: 38.7 us -> 39 us (level)
  Pallas kernels: 35.3 us -> 36.3 us
  local copies, waits for them, and re-layouts: 1.27 us -> 0.62 us
    pallas_call x1, Pallas kernels: 28.1 us -> 29.1 us  [fast_body(): pl.pallas_call(functools.partial(attention_kernel, row_count, col_count,...]
    pad x1 -> x0, local copies, waits for them, and re-layouts: 0.6 us -> none  [fast_body(): bias_w = jnp.pad(bias_weight.T, ((0, tile_heads - head_count), (0, 0)))]
where the time goes in v4:
time: 39 us; the launch traced here: 38.8 us
  Pallas kernels  36.3 us (93%)
  between operations  1.3 us (3%)
  other arithmetic  0.62 us (2%)
  local copies, waits for them, and re-layouts  0.62 us (2%)
    pallas_call x1, Pallas kernels, fast_body(): pl.pallas_call(functools.partial(attention_kernel, row_count, col_count,...  29.1 us
    pallas_call x1, Pallas kernels, fast_body(): pl.pallas_call(pair_kernel, grid=(rows // block,), out_shape=jax.ShapeDty...  7.14 us

profile of v4, /device:TPU:0, one launch (start us, length us, event | category | flops | bytes accessed | tf_op | source)
XLA Modules:
  0.0 38.8 jit_solution(12056979449095826804)
XLA Ops:
  1.3 0.6 %maximum_convert_fusion.embedded_ref = f32[1,256]{1,0:T(1,128)} fusion(bf16[1,128]{1,0:T(2,128)(2,1)S(1)} %get-tuple-element.8, bf16[1,128]{1,0:T(2,128)(2,1)S(1)} %get-tuple-element.9), kind=kLoop, calls=%fused_computation | loop fusion | flops 1024 | bytes 1536 | tf_op jit(solution)/shard_map/convert_element_type | solution.py:761
  1.9 29.1 %attention.1 = (bf16[64,192]{1,0:T(8,128)(2,1)}, f32[64,32,128]{2,1,0:T(8,128)}, bf16[64,128]{1,0:T(8,128)(2,1)}) custom-call(bf16[64,192]{1,0:T(8,128)(2,1)} %single_ref.1, f32[1,256]{1,0:T(1,128)} %maximum_convert_fusion.embedded_ref, bf16[192,256]{1,0:T(8,128)(2,1)} %bitcast.26, bf16[192,256]{1,0:T(8,128)(2,1)} %bitcast.27, s32[1,256]{1,0:T(1,128)} %bitcast.32, ...), custom_call_target="tpu_custom_call" | custom-call | tf_op jit(solution)/shard_map/attention/pallas_call | solution.py:721
  31.0 0.0 copy-start
  31.0 7.1 %transition.1 = bf16[64,64,128]{2,1,0:T(8,128)(2,1)} custom-call(s32[256]{0:T(256)} %live_ref.1, bf16[64,64,128]{2,1,0:T(8,128)(2,1)} %pair_ref.1, f32[64,32,128]{2,1,0:T(8,128)} %get-tuple-element.6.mix_ref, bf16[64,128]{1,0:T(8,128)(2,1)} %get-tuple-element.7.right_ref, f32[1,128]{1,0:T(1,128)} %bitcast.35, f32[1,128]{1,0:T(1,128)} %bitcast.36, ...), custom_call_target="tpu_custom_call" | custom-call | tf_op jit(solution)/shard_map/transition/pallas_call | solution.py:782
  38.2 0.0 copy-done
  38.2 0.6 %copy.27 = bf16[64,192]{1,0:T(8,128)(2,1)} copy(bf16[64,192]{1,0:T(8,128)(2,1)S(1)} %copy-done) | data formatting | bytes 49152
  (1 shorter events, 0.0 us)
Async XLA Ops:
  31.0 7.2 %copy-start = (bf16[64,192]{1,0:T(8,128)(2,1)S(1)}, bf16[64,192]{1,0:T(8,128)(2,1)}, u32[]{:S(2)}) copy-start(bf16[64,192]{1,0:T(8,128)(2,1)} %get-tuple-element.12) | copy-start | bytes 73732
